TPU v7x, 32 devices: a whole 2x2x4 slice. The times are simulated.
32 devices in a mesh: dp: 8 (over z, x), blk: 4 (over y, core).
Axes of the slice: x: 2, y: 2, z: 4, core: 2. Of those that a mesh axis runs over, the one named last changes fastest.
Arguments:
- block_input: float32 [73728, 512], P('dp', 'blk'), may hold values from -6 to 6
- cotangent: float32 [73728, 512], P('dp', 'blk'), may hold values from -6 to 6
- item_sides: int32 [8], P('dp'), may hold values from 48 to 96, as said below
- item_modes: int32 [8], P('dp'), may hold values from 12 to 32, as said below
- ln1_gain: float32 [512], P('blk'), may hold values from 0.1 to 1.9
- ln1_bias: float32 [512], P('blk'), may hold values from -3 to 3
- spec_w1: float32 [2, 8, 64, 64], P(None, 'blk'), may hold values from -0.5 to 0.5
- spec_b1: float32 [2, 8, 64], P(None, 'blk'), may hold values from -3 to 3
- spec_w2: float32 [2, 8, 64, 64], P(None, 'blk'), may hold values from -0.5 to 0.5
- spec_b2: float32 [2, 8, 64], P(None, 'blk'), may hold values from -3 to 3
- ln2_gain: float32 [512], P('blk'), may hold values from 0.1 to 1.9
- ln2_bias: float32 [512], P('blk'), may hold values from -3 to 3
- mlp_w1: float32 [512, 2048], P(None, 'blk'), may hold values from -0.25 to 0.25
- mlp_b1: float32 [2048], P('blk'), may hold values from -3 to 3
- mlp_w2: float32 [2048, 512], P('blk'), may hold values from -0.125 to 0.125
- mlp_b2: float32 [512], P('blk'), may hold values from -3 to 3
Outputs:
- block_output: float32 [73728, 512], P('dp', 'blk')
- input_grad: float32 [73728, 512], P('dp', 'blk')
- ln1_gain_grad: float32 [512], P('blk')
- ln1_bias_grad: float32 [512], P('blk')
- spec_w1_grad: float32 [2, 8, 64, 64], P(None, 'blk')
- spec_b1_grad: float32 [2, 8, 64], P(None, 'blk')
- spec_w2_grad: float32 [2, 8, 64, 64], P(None, 'blk')
- spec_b2_grad: float32 [2, 8, 64], P(None, 'blk')
- ln2_gain_grad: float32 [512], P('blk')
- ln2_bias_grad: float32 [512], P('blk')
- mlp_w1_grad: float32 [512, 2048], P(None, 'blk')
- mlp_b1_grad: float32 [2048], P('blk')
- mlp_w2_grad: float32 [2048, 512], P('blk')
- mlp_b2_grad: float32 [512], P('blk')
Inputs may be any that keep to these rules, and one draw needn't show every extreme that they name: `item_sides`: each item's side is 48, 72 or 96; at least one item has side 96. `item_modes`: an item of side s keeps m between max(1, s // 4) and min(32, s // 2); an item of side 96 with m = 32 is present.
All inputs are finite; a program needn't handle non-finite values.
Results may differ from a plain program's by a relative error of at most 0.0028.
Values sent between devices are 32-bit elements; how exact they have to be, the bound alone decides.
No kernel may reach another device: no remote copies, remote signals or barrier semaphores. Data moves between devices by JAX's collectives and lax.ppermute only.
A program may use at most 320 MiB of HBM per device.

v0:
```python
import functools
import math

import jax
import jax.numpy as jnp
from jax import lax
from jax.experimental import pallas as pl
from jax.experimental.pallas import tpu as pltpu
from jax.sharding import PartitionSpec as P

C = 512
MODES = 32
SMAX = 96
LANES = 128
FREQ = 64
HALF = 32
PARTS = 4
CHUNKS = 3
SLABS = SMAX // (PARTS * CHUNKS)
PIECE = SLABS * SMAX
GROUP = PARTS * SLABS
STEPS = SMAX // SLABS
STAGE = 24
THIRDS = STAGE // SLABS
WIDTH = 8
BATCH = 8
TILE = 256
SUB = 768
HID = 512
PACK = 4 * FREQ + 8

EPS = 1e-05
SHRINK = 0.01
F32 = jnp.float32
BF16 = jnp.bfloat16
NN = (((1,), (0,)), ((), ()))
NT = (((1,), (1,)), ((), ()))
TN = (((0,), (0,)), ((), ()))
LIMIT = 56 * 1024 * 1024


def mm(left, right, dims=NN):
    return lax.dot_general(left, right, dims, preferred_element_type=F32)


def split2(value):
    high = value.astype(BF16)
    return high, (value - high.astype(F32)).astype(BF16)


def split3(value):
    high = value.astype(BF16)
    rest = value - high.astype(F32)
    mid = rest.astype(BF16)
    return high, mid, (rest - mid.astype(F32)).astype(BF16)


def left6(value):
    one, two, three = split3(value)
    return jnp.concatenate([one, one, two, one, two, three], axis=1)


def right6(value):
    one, two, three = split3(value)
    return jnp.concatenate([one, two, one, three, two, one], axis=0)


def left3(value):
    one, two = split2(value)
    return jnp.concatenate([one, one, two], axis=1)


def right3(value):
    one, two = split2(value)
    return jnp.concatenate([one, two, one], axis=0)


def phi_pair(value):
    cdf = 0.5 + 0.5 * lax.erf(value * math.sqrt(0.5))
    pdf = jnp.exp(value * value * -0.5) * (1.0 / math.sqrt(2.0 * math.pi))
    return cdf, pdf


def pad_rows(value):
    return jnp.concatenate([value, jnp.zeros((LANES - SMAX, value.shape[1]), F32)], axis=0)


def fold_rows(value):
    return jnp.sum(value.reshape(-1, 8, value.shape[-1]), axis=0)


def spread8(rows):
    one, two, three = split3(rows)
    parts = [value.astype(F32) for value in (one, two, three)]
    left = jnp.concatenate(parts + [jnp.zeros_like(rows)], axis=0).astype(BF16)
    index = lax.broadcasted_iota(jnp.int32, (32, SLABS * LANES), 0)
    lane = lax.broadcasted_iota(jnp.int32, (32, SLABS * LANES), 1)
    pick = (index % SLABS == lane // LANES) & (index < 3 * SLABS)
    return mm(left, jnp.where(pick, 1.0, 0.0).astype(BF16), TN)


def slab_of(wide, slab):
    return wide[:SMAX, slab * LANES : (slab + 1) * LANES]


def us(time):
    return (int(time * 1e9), int(time * 3e6))


def call(body, out_shape, in_specs, out_specs, grid=(), scratch=(), aliases=None, cost=None):
    flops, moved = cost or (0, 0)
    return pl.pallas_call(
        body,
        out_shape=out_shape,
        grid=grid,
        in_specs=in_specs,
        out_specs=out_specs,
        scratch_shapes=list(scratch),
        input_output_aliases=aliases or {},
        compiler_params=pltpu.CompilerParams(vmem_limit_bytes=LIMIT),
        cost_estimate=pl.CostEstimate(flops=flops, bytes_accessed=moved, transcendentals=0),
    )


SMEM = pl.BlockSpec(memory_space=pltpu.SMEM)
VMEM = pl.BlockSpec(memory_space=pltpu.VMEM)
ANY = pl.BlockSpec(memory_space=pl.ANY)


def whole(shape):
    zeros = (0,) * len(shape)
    return pl.BlockSpec(shape, lambda *_: zeros)


def sds(shape, dtype=F32):
    return jax.ShapeDtypeStruct(shape, dtype)


def table(item_sides, item_modes):
    row = lax.broadcasted_iota(jnp.int32, (LANES, LANES), 0)
    cell = lax.broadcasted_iota(jnp.int32, (LANES, LANES), 1)
    index = row % FREQ
    frequency = index - (MODES - 1)
    extent = item_sides[0]
    phase = frequency * cell % extent
    keep = (jnp.abs(frequency) < item_modes[0]) & (cell < extent) & (index < 2 * MODES - 1)
    length = extent.astype(F32)
    angle = 2.0 * math.pi * phase.astype(F32) / length
    wave = jnp.where(row < FREQ, jnp.cos(angle), -jnp.sin(angle)) * lax.rsqrt(length)
    return jnp.where(keep, wave, jnp.zeros_like(wave))


def big_weight(weight, out):
    out[...] = jnp.zeros_like(out)
    for block in range(2):
        rows = pl.ds(block * 64, 64)
        later = pl.ds(128 + block * 64, 64)
        out[rows, rows] = weight[0, block]
        out[rows, later] = weight[1, block]
        out[later, rows] = -weight[1, block]
        out[later, later] = weight[0, block]


def prepare_body(f_ref, w1_ref, w2_ref, f6, g6, ft3, gt3, w1c, w2c, w1t, w2t, big):
    full = f_ref[...]
    cosine, sine = full[:FREQ], full[FREQ:]
    half = jnp.concatenate([cosine[HALF - 1 : FREQ - 1], sine[HALF - 1 : FREQ - 1]], axis=0)
    f6[...] = left6(half)
    ft3[...] = left3(half.T)
    lines = [(cosine, -sine), (sine, cosine), (cosine, sine), (sine, -cosine)]
    table_ = jnp.concatenate([jnp.concatenate(line, axis=1) for line in lines], axis=0)
    g6[...] = left6(table_)
    gt3[...] = left3(table_.T)
    for source, straight, across in ((w1_ref, w1c, w1t), (w2_ref, w2c, w2t)):
        big_weight(source, big)
        straight[...] = right6(big[...])
        across[...] = right3(big[...].T)


def prepare(forward, spec_w1, spec_w2):
    shapes = [
        sds((64, 768), BF16),
        sds((256, 1536), BF16),
        sds((128, 192), BF16),
        sds((256, 768), BF16),
        sds((1536, 256), BF16),
        sds((1536, 256), BF16),
        sds((768, 256), BF16),
        sds((768, 256), BF16),
    ]
    return call(
        prepare_body,
        shapes,
        [VMEM] * 3,
        [VMEM] * 8,
        scratch=[pltpu.VMEM((256, 256), F32)],
        cost=us(3),
    )(forward, spec_w1, spec_w2)


def slab_mask(first, side):
    cell = lax.broadcasted_iota(jnp.int32, (SMAX, LANES), 0)
    return (cell < side) & (first < side)


def moments_body(side_ref, x_ref, b1_ref, gain_ref, bias_ref, out_ref):
    step = pl.program_id(0)
    side = side_ref[0]

    @pl.when(step == 0)
    def _():
        vectors = [b1_ref[...], gain_ref[...], bias_ref[...], jnp.zeros((2, LANES), F32)]
        out_ref[2 * STEPS] = jnp.concatenate(vectors, axis=0)

    for slab in range(STAGE):
        inside = slab_mask(step * STAGE + slab, side)
        value = pad_rows(jnp.where(inside, x_ref[slab], 0.0)).T
        mean = jnp.sum(value, axis=0, keepdims=True) * (1.0 / LANES)
        centered = value - mean
        block, row = step * THIRDS + slab // SLABS, pl.ds(slab % SLABS, 1)
        out_ref[block, row, :] = mean
        out_ref[STEPS + block, row, :] = jnp.sum(centered * centered, axis=0, keepdims=True)


def moments(side, x, b1, gain, bias):
    return call(
        moments_body,
        sds((2 * STEPS + 1, SLABS, LANES)),
        [
            SMEM,
            pl.BlockSpec((STAGE, SMAX, LANES), lambda i: (i, 0, 0)),
            whole((4, LANES)),
            whole((1, LANES)),
            whole((1, LANES)),
        ],
        whole((2 * STEPS + 1, SLABS, LANES)),
        grid=(SMAX // STAGE,),
        cost=us(6),
    )(side, x, b1, gain, bias)


def cotangent_body(side_ref, g_ref, early, late, total):
    chunk = pl.program_id(0)
    side = side_ref[0]

    @pl.when(chunk == 0)
    def _():
        total[...] = jnp.zeros_like(total)

    def emit(out_ref):
        carry = jnp.zeros((8, LANES), F32)
        for part in range(PARTS):
            for slab in range(SLABS):
                first = part * SLABS + slab
                value = jnp.where(slab_mask(chunk * GROUP + first, side), g_ref[first], 0.0)
                out_ref[part, 0, slab] = value
                carry = carry + fold_rows(value)
        total[...] += carry

    @pl.when(chunk < CHUNKS - 1)
    def _():
        emit(early)

    @pl.when(chunk == CHUNKS - 1)
    def _():
        emit(late)


def cotangent_pieces(side, g):
    block = (PARTS, 1, SLABS, SMAX, LANES)
    return call(
        cotangent_body,
        [sds((PARTS, CHUNKS - 1, SLABS, SMAX, LANES)), sds(block), sds((8, LANES))],
        [SMEM, pl.BlockSpec((GROUP, SMAX, LANES), lambda i: (i, 0, 0))],
        [
            pl.BlockSpec(block, lambda i: (0, jnp.minimum(i, CHUNKS - 2), 0, 0, 0)),
            whole(block),
            whole((8, LANES)),
        ],
        grid=(CHUNKS,),
        cost=us(5),
    )(side, g)


def row_stats(means, totals):
    mean = (means[0] + means[1] + means[2] + means[3]) * (1.0 / PARTS)
    total = totals[0] + totals[1] + totals[2] + totals[3]
    for part in range(PARTS):
        gap = means[part] - mean
        total = total + LANES * (gap * gap)
    spread_ = total * (1.0 / C) + EPS
    inverse = lax.rsqrt(spread_)
    inverse = inverse * (1.5 - 0.5 * spread_ * inverse * inverse)
    return mean, inverse


def first_body(side_ref, x_ref, *refs):
    stats = refs[:PARTS]
    gain_ref, bias_ref, f6_ref, b_ref, xn_ref, xhat_ref, r_ref = refs[PARTS:]
    step = pl.program_id(0)
    side = side_ref[0]
    gain, bias = gain_ref[...], bias_ref[...]
    for third in range(THIRDS):
        block = step * THIRDS + third
        mean, inverse = row_stats([ref[block] for ref in stats], [ref[STEPS + block] for ref in stats])
        r_ref[pl.ds(third * SLABS, SLABS), :] = inverse
        means, scales = spread8(mean), spread8(inverse)
        columns = []
        for inner in range(SLABS):
            slab = third * SLABS + inner
            value = jnp.where(slab_mask(step * STAGE + slab, side), x_ref[slab], 0.0)
            centered = value - slab_of(means, inner)
            normal = centered * slab_of(scales, inner)
            normed = normal * gain + bias
            xhat_ref[slab] = normal
            xn_ref[slab] = value + normed
            columns.append(pad_rows(normed))
        out = mm(f6_ref[...], right6(jnp.concatenate(columns, axis=1)))
        for inner in range(SLABS):
            b_ref[third * SLABS + inner] = out[:, part_lanes(inner)]


def first_stage(side, x, stats, gain, bias, f6):
    field = pl.BlockSpec((STAGE, SMAX, LANES), lambda i: (i, 0, 0))
    return call(
        first_body,
        [sds((SMAX, FREQ, LANES)), sds((SMAX, SMAX, LANES)), sds((SMAX, SMAX, LANES)), sds((SMAX, LANES))],
        [SMEM, field]
        + [whole((2 * STEPS + 1, SLABS, LANES))] * PARTS
        + [whole((1, LANES)), whole((1, LANES)), whole((64, 768))],
        [
            pl.BlockSpec((STAGE, FREQ, LANES), lambda i: (i, 0, 0)),
            field,
            field,
            pl.BlockSpec((STAGE, LANES), lambda i: (i, 0)),
        ],
        grid=(SMAX // STAGE,),
        cost=us(3),
    )(side, x, *stats, gain, bias, f6)


def gather_columns(re_ref, im_ref, first):
    zeros = jnp.zeros((LANES - SMAX, LANES), F32)
    re, im = [ref.reshape(SMAX * WIDTH, LANES) for ref in (re_ref, im_ref)]
    columns = []
    for j in range(first, first + BATCH):
        rows = pl.ds(j, SMAX, stride=WIDTH)
        columns.append(jnp.concatenate([re[rows, :], zeros, im[rows, :], zeros], axis=0))
    return jnp.concatenate(columns, axis=1)


def to_rows(out):
    rows = []
    for j in range(BATCH):
        lanes = part_lanes(j)
        for base in (0, 2 * FREQ):
            parts = [out[base : base + FREQ, lanes], out[base + FREQ : base + 2 * FREQ, lanes]]
            rows.append(jnp.concatenate(parts, axis=1))
    return jnp.concatenate(rows, axis=0)


def to_columns(rows):
    columns = []
    for j in range(BATCH):
        parts = []
        for sign in range(2):
            first = (2 * j + sign) * FREQ
            part = rows[first : first + FREQ]
            parts += [part[:, :LANES], part[:, LANES:]]
        columns.append(jnp.concatenate(parts, axis=0))
    return jnp.concatenate(columns, axis=1)


def counted(step, half, shape):
    row = lax.broadcasted_iota(jnp.int32, shape, 0)
    twice = (step == 0) & (half == 0)
    return (row < FREQ) | (row >= 2 * FREQ) | jnp.logical_not(twice)


def scatter_columns(re_ref, im_ref, first, out):
    re, im = [ref.reshape(SMAX * WIDTH, LANES) for ref in (re_ref, im_ref)]
    for j in range(BATCH):
        lanes = slice(j * LANES, (j + 1) * LANES)
        rows = pl.ds(first + j, SMAX, stride=WIDTH)
        re[rows, :] = out[:SMAX, lanes]
        im[rows, :] = out[LANES : LANES + SMAX, lanes]


def shrink(value):
    return jnp.where(
        value > SHRINK,
        value - SHRINK,
        jnp.where(value < -SHRINK, value + SHRINK, jnp.zeros_like(value)),
    )


def mix_body(re_ref, im_ref, g6_ref, w1_ref, b1_ref, w2_ref, b2_ref, gt3_ref, bre, bim, a_out, p_out, o_out):
    for half in range(WIDTH // BATCH):
        rows = pl.ds(half * 2 * BATCH * FREQ, 2 * BATCH * FREQ)
        spectrum = to_rows(mm(g6_ref[...], right6(gather_columns(re_ref, im_ref, BATCH * half))))
        a_out[rows, :] = spectrum
        pre = mm(left6(spectrum), w1_ref[...]) + b1_ref[...]
        p_out[rows, :] = pre
        cdf = 0.5 + 0.5 * lax.erf(pre * math.sqrt(0.5))
        out = mm(left6(pre * cdf), w2_ref[...]) + b2_ref[...]
        o_out[rows, :] = out
        if half == 0:
            out = jnp.where(counted(pl.program_id(0), half, out.shape), out, 0.0)
        scatter_columns(bre, bim, BATCH * half, mm(gt3_ref[...], right3(to_columns(shrink(out)))))


def mix_forward(b, g6, w1c, bias1, w2c, bias2, gt3):
    count = HALF // WIDTH
    re = pl.BlockSpec((SMAX, WIDTH, LANES), lambda j: (0, j, 0))
    im = pl.BlockSpec((SMAX, WIDTH, LANES), lambda j: (0, count + j, 0))
    out = pl.BlockSpec((SMAX, WIDTH, LANES), lambda j: (0, j, 0))
    rows = pl.BlockSpec((2 * WIDTH * FREQ, 256), lambda j: (j, 0))
    half = sds((SMAX, HALF, LANES))
    return call(
        mix_body,
        [half, half] + [sds((4096, 256))] * 3,
        [
            re,
            im,
            whole((256, 1536)),
            whole((1536, 256)),
            whole((1, 256)),
            whole((1536, 256)),
            whole((1, 256)),
            whole((256, 768)),
        ],
        [out, out, rows, rows, rows],
        grid=(count,),
        cost=us(0.1),
    )(b, b, g6, w1c, bias1, w2c, bias2, gt3)


def last_body(own_ref, re_ref, im_ref, xn_ref, ft3_ref, *refs):
    full, outs = refs[-1], refs[-1 - PARTS : -1]
    own = own_ref[0]
    for part in range(PARTS):
        base = (own ^ part) * SLABS
        columns = [jnp.concatenate([re_ref[base + s], im_ref[base + s]], axis=0) for s in range(SLABS)]
        out = mm(ft3_ref[...], right3(jnp.concatenate(columns, axis=1)))[:SMAX]
        for s in range(SLABS):
            value = xn_ref[base + s] + out[:, part_lanes(s)]
            full[base + s] = value
            if len(outs[part].shape) == 3:
                outs[part][s] = value
            else:
                outs[part][0, s] = value


def last_stage(own, bre, bim, xn, ft3, keep, chunk):
    half = pl.BlockSpec((GROUP, HALF, LANES), lambda i: (chunk + i, 0, 0))
    field = pl.BlockSpec((GROUP, SMAX, LANES), lambda i: (chunk + i, 0, 0))
    args = [own, bre, bim, xn, ft3]
    in_specs = [SMEM, half, half, field, whole((128, 192))]
    aliases = {}
    steps = 1 if chunk == 0 else CHUNKS - 1
    if keep is not None:
        aliases[len(args)] = PARTS
        args.append(keep)
        in_specs.append(ANY)
    piece = (SLABS, SMAX, LANES)
    shape = piece if chunk == 0 else (steps,) + piece
    spec = whole(piece)
    if chunk > 0:
        spec = pl.BlockSpec((1,) + piece, lambda i: (i, 0, 0, 0))
    *pieces, full = call(
        last_body,
        [sds(shape)] * PARTS + [sds((SMAX, SMAX, LANES))],
        in_specs,
        [spec] * PARTS + [field],
        grid=(steps,),
        aliases=aliases,
        cost=us(0.1 * steps),
    )(*args)
    return pieces, full


def weights_body(own_ref, *refs):
    own = own_ref[0]
    firsts, seconds, outs = refs[:PARTS], refs[PARTS : 2 * PARTS], refs[2 * PARTS :]
    w1h, w1l, w2h, w2l = outs
    for block in range(PARTS):
        w1h[block], w1l[block] = split2(firsts[block][...].reshape(LANES, HID))
        for part in range(PARTS):
            source = pl.ds(pl.multiple_of((own ^ part) * LANES, LANES), LANES)
            ref = seconds[block]
            value = ref[:, source] if len(ref.shape) == 2 else ref[:, 0, :, source].reshape(LANES, LANES)
            high, low = split2(value)
            w2h[block, :, part_lanes(part)] = high
            w2l[block, :, part_lanes(part)] = low


def split_weights(own, one, two, far):
    depth, height = far[0].shape[0] // PARTS, far[0].shape[2]
    far_block = (depth, 1, height, HID)
    turned = pl.BlockSpec((LANES, HID), lambda i, own_ref: (i ^ own_ref[0], 0))
    straight = pl.BlockSpec((LANES, HID), lambda i, own_ref: (i, 0))
    far_turned = pl.BlockSpec(far_block, lambda i, own_ref: (i ^ own_ref[0], 0, 0, 0))
    far_straight = pl.BlockSpec(far_block, lambda i, own_ref: (i, 1, 0, 0))
    flops, moved = us(0.1)
    return pl.pallas_call(
        weights_body,
        out_shape=[sds((4, 512, 512), BF16)] * 4,
        grid_spec=pltpu.PrefetchScalarGridSpec(
            num_scalar_prefetch=1,
            grid=(PARTS,),
            in_specs=[turned] * 2 + [far_turned] * 2 + [straight] * 2 + [far_straight] * 2,
            out_specs=[pl.BlockSpec((PARTS, LANES, HID), lambda i, own_ref: (0, i, 0))] * 4,
        ),
        compiler_params=pltpu.CompilerParams(vmem_limit_bytes=LIMIT),
        cost_estimate=pl.CostEstimate(flops=flops, bytes_accessed=moved, transcendentals=0),
    )(own, *one, *far, *two, *far)


def row_mean(parts):
    total = parts[0] + parts[1] + parts[2] + parts[3]
    return jnp.sum(total, axis=1, keepdims=True) * (1.0 / C)


def part_lanes(part):
    return slice(part * LANES, (part + 1) * LANES)


def norm_tiles(load, vectors, n_h, n_l, nh, nl, xhat, scale):
    def norm(tile, carry):
        rows = pl.ds(tile * TILE, TILE)
        values = [load(part, rows) for part in range(PARTS)]
        mean = row_mean(values)
        centered = [value - mean for value in values]
        spread_ = row_mean([value * value for value in centered]) + EPS
        inverse = lax.rsqrt(spread_)
        inverse = inverse * (1.5 - 0.5 * spread_ * inverse * inverse)
        scale[rows, :] = jnp.broadcast_to(inverse, (TILE, LANES))
        for part in range(PARTS):
            lanes = part_lanes(part)
            normal = centered[part] * inverse
            xhat[rows, lanes] = normal
            gain, bias = vectors[part][0, 4:5, :], vectors[part][0, 5:6, :]
            high, low = split2(normal * gain + bias)
            n_h[rows, lanes] = high
            n_l[rows, lanes] = low
            nh[rows, lanes] = high
            nl[rows, lanes] = low
        return carry

    lax.fori_loop(0, PIECE // TILE, norm, 0)


def bias_of(vectors, step):
    row = jnp.zeros((4, LANES), F32)
    for part in range(PARTS):
        row = jnp.where(step == part, vectors[part][0, 0:4, :], row)
    return jnp.concatenate([row[i : i + 1] for i in range(4)], axis=1)


def grad_tiles(own, g_ref, vectors, dn, xhat, scale, store, small):
    small[...] = jnp.zeros_like(small)

    def back(tile, carry):
        rows = pl.ds(tile * TILE, TILE)
        inverse = scale[rows, :]
        scaled, normals = [], []
        for part in range(PARTS):
            lanes = part_lanes(part)
            grad = dn[rows, lanes]
            normal = xhat[rows, lanes]
            small[0, :, lanes] += fold_rows(grad * normal)
            small[1, :, lanes] += fold_rows(grad)
            scaled.append(grad * vectors[part][0, 4:5, :])
            normals.append(normal)
        first = row_mean(scaled)
        second = row_mean([s * n for s, n in zip(scaled, normals)])
        for part in range(PARTS):
            delta = inverse * (scaled[part] - first - normals[part] * second)
            store(part, rows, g_ref[own ^ part, rows, :] + delta)
        return carry

    lax.fori_loop(0, PIECE // TILE, back, 0)


def split_cotangent(own, g_ref, g_h, g_l):
    for part in range(PARTS):
        lanes = part_lanes(part)
        g_h[:, lanes], g_l[:, lanes] = split2(g_ref[own ^ part])


def product3(high, low, w_h, w_l, dims=NN):
    return mm(high, w_h[0], dims) + mm(low, w_h[0], dims) + mm(high, w_l[0], dims)


def add_to(ref, step, value):
    ref[...] = jnp.where(step == 0, 0.0, ref[...]) + value


def feed_body(*refs):
    own = refs[0][0]
    x_refs, g_ref = refs[1:5], refs[5]
    w1h, w1l, w2h, w2l = refs[6:10]
    vectors = refs[10:14]
    refs = refs[len(refs) - 21 :]
    hh, hl, nh, nl, out_ref, ph, plo = refs[0:7]
    dx_refs, db1, small = refs[7:11], refs[11], refs[12]
    n_h, n_l, g_h, g_l, xhat, scale, dn, acc = refs[13:21]
    step = pl.program_id(0)

    @pl.when(step == 0)
    def _():
        norm_tiles(lambda part, rows: x_refs[part][rows, :], vectors, n_h, n_l, nh, nl, xhat, scale)
        split_cotangent(own, g_ref, g_h, g_l)

    pre = product3(n_h[...], n_l[...], w1h, w1l) + bias_of(vectors, step)
    dh = product3(g_h[...], g_l[...], w2h, w2l, NT)
    cdf, pdf = phi_pair(pre)
    high, low = split2(pre * cdf)
    hh[...] = high
    hl[...] = low
    grad = dh * (cdf + pre * pdf)
    add_to(acc, step, product3(high, low, w2h, w2l))
    high, low = split2(grad)
    ph[...] = high
    plo[...] = low
    db1[0] = fold_rows(grad)
    add_to(dn, step, product3(high, low, w1h, w1l, NT))

    @pl.when(step == pl.num_programs(0) - 1)
    def _():
        for part in range(PARTS):
            out_ref[own ^ part, 0] = acc[:, part_lanes(part)]

        def store(part, rows, value):
            dx_refs[part][rows, :] = value

        grad_tiles(own, g_ref, vectors, dn, xhat, scale, store, small)


def forward_body(*refs):
    own = refs[0][0]
    x_refs = refs[1:5]
    w1h, w1l, w2h, w2l = refs[5:9]
    vectors = refs[9:13]
    hh, hl, nh, nl, out_ref, slope, xhat, scale, n_h, n_l, acc = refs[len(refs) - 11 :]
    step = pl.program_id(0)

    @pl.when(step == 0)
    def _():
        norm_tiles(lambda part, rows: x_refs[part][rows, :], vectors, n_h, n_l, nh, nl, xhat, scale)

    pre = product3(n_h[...], n_l[...], w1h, w1l) + bias_of(vectors, step)
    cdf, pdf = phi_pair(pre)
    slope[...] = cdf + pre * pdf
    high, low = split2(pre * cdf)
    hh[...] = high
    hl[...] = low
    add_to(acc, step, product3(high, low, w2h, w2l))

    @pl.when(step == pl.num_programs(0) - 1)
    def _():
        for part in range(PARTS):
            out_ref[own ^ part, 0] = acc[:, part_lanes(part)]


def backward_body(*refs):
    own = refs[0][0]
    g_ref, w1h, w1l, w2h, w2l, slope, xhat, scale = refs[1:9]
    vectors = refs[9:13]
    refs = refs[len(refs) - 11 :]
    ph, plo, dx_refs, db1, small = refs[0], refs[1], refs[2:6], refs[6], refs[7]
    g_h, g_l, dn = refs[8:]
    step = pl.program_id(0)

    @pl.when(step == 0)
    def _():
        split_cotangent(own, g_ref, g_h, g_l)

    grad = product3(g_h[...], g_l[...], w2h, w2l, NT) * slope[...]
    high, low = split2(grad)
    ph[...] = high
    plo[...] = low
    db1[0] = fold_rows(grad)
    add_to(dn, step, product3(high, low, w1h, w1l, NT))

    @pl.when(step == pl.num_programs(0) - 1)
    def _():

        def store(part, rows, value):
            dx_refs[part][rows, :] = value

        grad_tiles(own, g_ref, vectors, dn, xhat, scale, store, small)


def feed_call(body, head, heads, weights, stats, local, keep, kinds, chunk, cost):
    rows = PIECE * CHUNKS
    specs = {
        "x": (sds((PIECE, LANES)), whole((PIECE, LANES))),
        "later": (None, pl.BlockSpec((PIECE, LANES), lambda i: (chunk - 1, 0))),
        "g": (None, pl.BlockSpec((PARTS, PIECE, LANES), lambda i: (0, chunk, 0))),
        "g2": (None, whole((PARTS, PIECE, LANES))),
        "out": (
            sds((PARTS, CHUNKS - 1, PIECE, LANES)),
            pl.BlockSpec((PARTS, 1, PIECE, LANES), lambda i: (0, chunk, 0, 0)),
        ),
        "wide": (sds((rows, 2048), BF16), pl.BlockSpec((PIECE, HID), lambda i: (chunk, i))),
        "narrow": (sds((rows, C), BF16), pl.BlockSpec((PIECE, C), lambda i: (chunk, 0))),
        "slope": (sds((PIECE, 2048)), pl.BlockSpec((PIECE, HID), lambda i: (0, i))),
        "tip": (sds((PARTS, 1, PIECE, LANES)), whole((PARTS, 1, PIECE, LANES))),
        "full": (sds((PIECE, C)), whole((PIECE, C))),
        "db1": (sds((4, 8, HID)), pl.BlockSpec((1, 8, HID), lambda i: (i, 0, 0))),
        "small": (sds((2, 8, C)), whole((2, 8, C))),
    }
    weight = pl.BlockSpec((1, 512, 512), lambda i: (i, 0, 0))
    vector = pl.BlockSpec((1, SLABS, LANES), lambda i: (2 * STEPS, 0, 0))
    args = [*head, *weights, *(value for _, value in local), *stats]
    in_specs = [SMEM] + [specs[kind][1] for kind in heads] + [weight] * 4
    in_specs += [specs[kind][1] for kind, _ in local] + [vector] * 4
    aliases = {}
    for index, array in enumerate(keep or ()):
        aliases[len(args)] = index
        args.append(array)
        in_specs.append(ANY)
    bf, big = pltpu.VMEM((PIECE, C), BF16), pltpu.VMEM((PIECE, C), F32)
    scratch = {
        "feed": [bf] * 4 + [big, pltpu.VMEM((PIECE, LANES), F32), big, big],
        "fore": [bf, bf, big],
        "back": [bf, bf, big],
    }[kinds]
    outs = {
        "feed": ["wide"] * 2 + ["narrow"] * 2 + ["out", "wide", "wide"] + ["x"] * 4 + ["db1", "small"],
        "fore": ["wide"] * 2 + ["narrow"] * 2 + ["tip", "slope", "full", "x"],
        "back": ["wide", "wide"] + ["x"] * 4 + ["db1", "small"],
    }[kinds]
    return call(
        body,
        [specs[kind][0] for kind in outs],
        in_specs,
        [specs[kind][1] for kind in outs],
        grid=(4,),
        scratch=scratch,
        aliases=aliases,
        cost=us(cost),
    )(*args)


def feed(own, xs, g, weights, stats, keep, chunk):
    head, heads = [own, *xs, g], ["x" if chunk == 0 else "later"] * 4 + ["g"]
    return feed_call(feed_body, head, heads, weights, stats, [], keep, "feed", chunk, 28)


def feed_forward(own, xs, weights, stats, keep, chunk):
    return feed_call(forward_body, [own, *xs], ["later"] * 4, weights, stats, [], keep, "fore", chunk, 18)


def feed_backward(own, g, weights, local, stats, keep, chunk):
    local = list(zip(("slope", "full", "x"), local))
    return feed_call(backward_body, [own, g], ["g2"], weights, stats, local, keep, "back", chunk, 16)


def weight_body(own_ref, place_ref, th, tl, *refs):
    send, held, t_h, t_l = refs[-4:]
    step = pl.program_id(0)
    own, place = own_ref[0], place_ref[0]

    @pl.when(step == 0)
    def _():
        if len(refs[0].shape) == 2:
            t_h[...] = refs[0][...].T
            t_l[...] = refs[1][...].T
        else:
            for part in range(PARTS):
                pieces = [ref[own ^ part] for ref in refs[:2]]
                high, low = split2(jnp.concatenate(pieces, axis=0))
                t_h[part_lanes(part), :] = high.T
                t_l[part_lanes(part), :] = low.T

    out = mm(t_h[...], th[...]) + mm(t_l[...], th[...]) + mm(t_h[...], tl[...])
    count, depth = send.shape[1], send.shape[2]

    def store(ref):
        for index in range(count):
            part, inner = divmod(index, count // PARTS)
            apart = ((own ^ part) * (count // PARTS) + inner) ^ place
            where = (apart & 1) * (count // 2) + (apart >> 1)
            ref[0, where] = out[index * depth : (index + 1) * depth]

    @pl.when(step < 2)
    def _():
        store(send)

    @pl.when(step >= 2)
    def _():
        store(held)


def weight_grads(own, place, dp_size, left, th, tl, cost):
    rows = PIECE * CHUNKS
    wide = pl.BlockSpec((rows, HID), lambda i: (0, (i % 2) * 2 + 1 - i // 2))
    block = (1, dp_size, C // dp_size, HID)
    shape = sds((2,) + block[1:])
    return call(
        weight_body,
        [shape, shape],
        [SMEM, SMEM]
        + [wide] * 2
        + [pl.BlockSpec(v.shape, lambda i, n=v.ndim: (0,) * n, pipeline_mode=pl.Buffered(1)) for v in left],
        [
            pl.BlockSpec(block, lambda i: (jnp.minimum(i, 1), 0, 0, 0)),
            pl.BlockSpec(block, lambda i: (jnp.maximum(i - 2, 0), 0, 0, 0)),
        ],
        grid=(4,),
        scratch=[pltpu.VMEM((C, rows), BF16)] * 2,
        cost=us(cost),
    )(own, place, th, tl, *left)


def assemble_body(turn, place_ref, near, far, out_ref, held):
    place = place_ref[0]
    half, depth = near.shape[0], near.shape[1]
    target = held if turn else out_ref
    for side, source in enumerate((near, far)):
        for index in range(half):
            rows = pl.ds(pl.multiple_of((place ^ (2 * index + side)) * depth, depth), depth)
            target[rows, :] = source[index]
    if turn:
        out_ref[...] = held[...].T


def assemble(place, near, far, turn):
    return call(
        functools.partial(assemble_body, turn),
        sds((C, HID)),
        [SMEM] + [VMEM] * 2,
        VMEM,
        scratch=[pltpu.VMEM((C, HID), F32)],
        cost=us(2),
    )(place, near, far)


def first_back_body(own_ref, f6_ref, *refs):
    d_ref, dx_ref = refs[-2:]
    own = own_ref[0]
    for chunk in range(CHUNKS):

        @pl.when(pl.program_id(0) == chunk)
        def _(pieces=refs[PARTS * chunk : PARTS * (chunk + 1)]):
            for part in range(PARTS):
                base = (own ^ part) * SLABS
                columns = [pad_rows(pieces[part][s]) for s in range(SLABS)]
                out = mm(f6_ref[...], right3(jnp.concatenate(columns, axis=1)))
                for s in range(SLABS):
                    d_ref[base + s] = out[:, part_lanes(s)]
                    dx_ref[base + s] = pieces[part][s]


def first_back(own, pieces, f6):
    return call(
        first_back_body,
        [sds((SMAX, FREQ, LANES)), sds((SMAX, SMAX, LANES))],
        [SMEM, whole((64, 384))] + [whole(piece.shape) for piece in pieces],
        [
            pl.BlockSpec((GROUP, FREQ, LANES), lambda i: (i, 0, 0)),
            pl.BlockSpec((GROUP, SMAX, LANES), lambda i: (i, 0, 0)),
        ],
        grid=(CHUNKS,),
        cost=us(8),
    )(own, f6, *pieces)


def rows3(value):
    one, two = split2(value)
    return jnp.concatenate([one, one, two], axis=0)


def mix_back_body(*refs):
    re_ref, im_ref, a_ref, p_ref, o_ref, g3_ref, w1t, w2t, gt3_ref = refs[:9]
    sums = refs[-4:]
    dw1, dw2, db1, db2 = sums
    if len(refs) == 15:
        dre, dim = refs[9:11]
    else:
        gb_ref = refs[13]
        dre, dim, pack = refs[14:17]

    @pl.when(pl.program_id(0) == 0)
    def _():
        for index, ref in enumerate(sums):
            ref[...] = jnp.zeros_like(ref) if len(refs) == 15 else refs[9 + index][...]

    for half in range(WIDTH // BATCH):
        rows = pl.ds(half * 2 * BATCH * FREQ, 2 * BATCH * FREQ)
        dz = to_rows(mm(g3_ref[...], right3(gather_columns(re_ref, im_ref, BATCH * half))))
        do = jnp.where(jnp.abs(o_ref[rows, :]) > SHRINK, dz, 0.0)
        if half == 0 and len(refs) == 15:
            do = jnp.where(counted(pl.program_id(0), half, do.shape), do, 0.0)
        pre = p_ref[rows, :]
        cdf, pdf = phi_pair(pre)
        dw2[...] += mm(rows3(pre * cdf), right3(do), TN)
        db2[...] += fold_rows(do)
        dp = mm(left3(do), w2t[...]) * (cdf + pre * pdf)
        dw1[...] += mm(rows3(a_ref[rows, :]), right3(dp), TN)
        db1[...] += fold_rows(dp)
        dx = mm(left3(dp), w1t[...])
        if half == 0 and len(refs) == 15:
            dx = jnp.where(counted(pl.program_id(0), half, dx.shape), dx, 0.0)
        scatter_columns(dre, dim, BATCH * half, mm(gt3_ref[...], right3(to_columns(dx))))

    if len(refs) == 15:
        return

    @pl.when(pl.program_id(0) == pl.num_programs(0) - 1)
    def _():
        low = lax.broadcasted_iota(jnp.int32, (FREQ, LANES), 1) < FREQ
        for index, ref in enumerate((dw1, dw2)):
            full = ref[...]
            same = full[:LANES, :LANES] + full[LANES:, LANES:]
            cross = full[:LANES, LANES:] - full[LANES:, :LANES]
            for inner, value in enumerate((same, cross)):
                rows = pl.ds((2 * index + inner) * FREQ, FREQ)
                pack[rows, :] = jnp.where(low, value[:FREQ], value[FREQ:])
        sums = [jnp.sum(ref[...], axis=0, keepdims=True) for ref in (db1, db2)]
        lines = [sums[0][:, :LANES], sums[0][:, LANES:], sums[1][:, :LANES], sums[1][:, LANES:]]
        lines.append(jnp.sum(gb_ref[...], axis=0, keepdims=True))
        pack[4 * FREQ : 4 * FREQ + 8] = jnp.concatenate(lines + [jnp.zeros((3, LANES), F32)], axis=0)


def mix_backward(d, a, p, o, g6, w1t, w2t, gt3, carry, grad_b2):
    count = HALF // WIDTH
    skip = 0 if carry is None else count // 2
    re = pl.BlockSpec((SMAX, WIDTH, LANES), lambda j: (0, skip + j, 0))
    im = pl.BlockSpec((SMAX, WIDTH, LANES), lambda j: (0, count + skip + j, 0))
    out = pl.BlockSpec((SMAX, WIDTH, LANES), lambda j: (0, j, 0))
    rows = pl.BlockSpec((2 * WIDTH * FREQ, 256), lambda j: (skip + j, 0))
    half = sds((SMAX, HALF // 2, LANES))
    args = [d, d, a, p, o, g6, w1t, w2t, gt3]
    in_specs = [re, im, rows, rows, rows, whole((256, 768))]
    in_specs += [whole((768, 256)), whole((768, 256)), whole((256, 768))]
    sums = [(256, 256), (256, 256), (8, 256), (8, 256)]
    shapes, out_specs, scratch = [half, half], [out, out], []
    if carry is None:
        shapes += [sds(shape) for shape in sums]
        out_specs += [whole(shape) for shape in sums]
    else:
        args += [*carry, grad_b2]
        in_specs += [whole(shape) for shape in sums] + [whole((8, LANES))]
        shapes.append(sds((PACK, LANES)))
        out_specs.append(whole((PACK, LANES)))
        scratch = [pltpu.VMEM(shape, F32) for shape in sums]
    return call(
        mix_back_body, shapes, in_specs, out_specs, grid=(count // 2,), scratch=scratch, cost=us(13)
    )(*args)


def last_back_body(re0, re1, im0, im1, dx_ref, xhat_ref, gain_ref, ft3_ref, pack_ref, *refs):
    b1_refs, norm_refs = refs[:CHUNKS], refs[CHUNKS : 2 * CHUNKS]
    dn_ref, pack = refs[2 * CHUNKS : 2 * CHUNKS + 2]
    sums, small = refs[-1 - PARTS : -1], refs[-1]
    step = pl.program_id(0)

    @pl.when(step == 0)
    def _():
        small[...] = jnp.zeros_like(small)
        norms = norm_refs[0][...]
        for ref in norm_refs[1:]:
            norms = norms + ref[...]
        norms = [jnp.sum(norms[i], axis=0, keepdims=True) for i in range(2)]
        for part in range(PARTS):
            total = b1_refs[0][part]
            for ref in b1_refs[1:]:
                total = total + ref[part]
            total = jnp.sum(total, axis=0, keepdims=True)
            lines = [total[:, part_lanes(i)] for i in range(4)]
            lines += [value[:, part_lanes(part)] for value in norms]
            lines.append(jnp.zeros((2, LANES), F32))
            sums[part][2 * STEPS] = jnp.concatenate(lines, axis=0)

    gain = gain_ref[...]
    for third in range(THIRDS):
        slabs = [third * SLABS + inner for inner in range(SLABS)]
        columns = [jnp.concatenate([re0[s], re1[s], im0[s], im1[s]], axis=0) for s in slabs]
        out = mm(ft3_ref[...], right3(jnp.concatenate(columns, axis=1)))[:SMAX]
        for index, s in enumerate(slabs):
            grad = dx_ref[s] + out[:, part_lanes(index)]
            dn_ref[s] = grad
            product = grad * xhat_ref[s]
            small[0] += fold_rows(product)
            small[1] += fold_rows(grad)
            for which, value in enumerate((grad, product)):
                row = jnp.sum(pad_rows(value * gain).T, axis=0, keepdims=True)
                for ref in sums:
                    block = which * STEPS + step * THIRDS + s // SLABS
                    ref[block, pl.ds(s % SLABS, 1), :] = row

    @pl.when(step == pl.num_programs(0) - 1)
    def _():
        pack[...] = pack_ref[...]
        for index in range(2):
            where = pl.ds(4 * FREQ + 5 + index, 1)
            pack[where, :] = jnp.sum(small[index], axis=0, keepdims=True)


def last_back(quarters, dx, xhat, gain, ft3, pack, b1s, norms):
    half = pl.BlockSpec((STAGE, HALF // 2, LANES), lambda i: (i, 0, 0))
    field = pl.BlockSpec((STAGE, SMAX, LANES), lambda i: (i, 0, 0))
    shape = (2 * STEPS + 1, SLABS, LANES)
    return call(
        last_back_body,
        [sds((SMAX, SMAX, LANES)), sds((PACK, LANES))] + [sds(shape)] * PARTS,
        [half] * 4
        + [field, field, whole((1, LANES)), whole((128, 192)), whole((PACK, LANES))]
        + [whole((4, 8, HID))] * CHUNKS
        + [whole((2, 8, C))] * CHUNKS,
        [field, whole((PACK, LANES))] + [whole(shape)] * PARTS,
        grid=(SMAX // STAGE,),
        scratch=[pltpu.VMEM((2, 8, LANES), F32)],
        cost=us(13),
    )(*quarters, dx, xhat, gain, ft3, pack, *b1s, *norms)


def final_body(side_ref, dx_ref, dn_ref, xhat_ref, r_ref, gain_ref, *refs):
    sums, out_ref = refs[:PARTS], refs[PARTS]
    step = pl.program_id(0)
    side = side_ref[0]
    for third in range(THIRDS):
        block = step * THIRDS + third
        inverse = r_ref[pl.ds(third * SLABS, SLABS), :]
        total = [sum(ref[which * STEPS + block] for ref in sums) for which in range(2)]
        first = total[0] * (inverse * (1.0 / C))
        second = total[1] * (inverse * (1.0 / C))
        wide = [spread8(value) for value in (inverse, first, second)]
        for inner in range(SLABS):
            slab = third * SLABS + inner
            scaled = dn_ref[slab] * gain_ref[...]
            scale, shift, slope = [slab_of(value, inner) for value in wide]
            value = dx_ref[slab] + (scale * scaled - shift - xhat_ref[slab] * slope)
            out_ref[slab] = jnp.where(slab_mask(step * STAGE + slab, side), value, 0.0)


def final_stage(side, dx, dn, xhat, sums, r, gain):
    field = pl.BlockSpec((STAGE, SMAX, LANES), lambda i: (i, 0, 0))
    return call(
        final_body,
        sds((SMAX, SMAX, LANES)),
        [SMEM, field, field, field, pl.BlockSpec((STAGE, LANES), lambda i: (i, 0)), whole((1, LANES))]
        + [whole((2 * STEPS + 1, SLABS, LANES))] * PARTS,
        field,
        grid=(SMAX // STAGE,),
        cost=us(13),
    )(side, dx, dn, xhat, r, gain, *sums)


def output_body(side_ref, x_ref, y_ref, tip_ref, b2_ref, out_ref):
    step = pl.program_id(0)
    side = side_ref[0]
    for part in range(PARTS):
        for inner in range(SLABS):
            slab = part * SLABS + inner
            branch = jnp.where(step < CHUNKS - 1, y_ref[part, 0, inner], tip_ref[part, inner])
            value = x_ref[slab] + branch + b2_ref[...]
            out_ref[slab] = jnp.where(slab_mask(step * GROUP + slab, side), value, 0.0)


def output_stage(side, x1, y, tip, b2):
    field = pl.BlockSpec((GROUP, SMAX, LANES), lambda i: (i, 0, 0))
    return call(
        output_body,
        sds((SMAX, SMAX, LANES)),
        [
            SMEM,
            field,
            pl.BlockSpec(
                (PARTS, 1, SLABS, SMAX, LANES), lambda i: (0, jnp.minimum(i, CHUNKS - 2), 0, 0, 0)
            ),
            whole((PARTS, SLABS, SMAX, LANES)),
            whole((1, LANES)),
        ],
        field,
        grid=(CHUNKS,),
        cost=us(5),
    )(side, x1, y, tip, b2)


def swap(value, axis, size, distance):
    return lax.ppermute(value, axis, [(i, i ^ distance) for i in range(size)])


def exchange(pieces):
    return [pieces[0]] + [swap(pieces[part], "blk", PARTS, part) for part in range(1, PARTS)]


def after(value, *others):
    return lax.optimization_barrier((value, *others))[0]


def halve(value, size, distance, gate):
    cut = value.shape[0] // 2
    return after(value[:cut], gate) + swap(value[cut:], "dp", size, distance)


def scatter_last(mine, size, gate):
    total = after(mine[0], gate)
    for index in range(1, size // 2):
        total = total + swap(mine[index], "dp", size, 2 * index)
    return total


def gather_near(piece, size, gate):
    return jnp.stack([after(piece, gate)] + [swap(piece, "dp", size, 2 * index) for index in range(1, size // 2)])


def per_device(
    dp_size,
    block_input,
    cotangent,
    item_sides,
    item_modes,
    ln1_gain,
    ln1_bias,
    spec_w1,
    spec_b1,
    spec_w2,
    spec_b2,
    ln2_gain,
    ln2_bias,
    mlp_w1,
    mlp_b1,
    mlp_w2,
    mlp_b2,
):
    own = lax.axis_index("blk").astype(jnp.int32).reshape(1)
    place = lax.axis_index("dp").astype(jnp.int32).reshape(1)
    cube = (SMAX, SMAX, LANES)
    x = block_input.reshape(cube)
    gain1, bias1 = ln1_gain.reshape(1, LANES), ln1_bias.reshape(1, LANES)

    depth = C // dp_size
    share = jnp.stack([lax.dynamic_slice_in_dim(w, place[0] * depth, depth) for w in (mlp_w1, mlp_w2)])
    share = swap(share, "blk", PARTS, 2)
    moment = moments(
        item_sides, x, mlp_b1.reshape(4, LANES), ln2_gain.reshape(1, LANES), ln2_bias.reshape(1, LANES)
    )
    stats = exchange([moment] * PARTS)
    g_parts, g_late, grad_b2 = cotangent_pieces(item_sides, after(cotangent.reshape(cube), moment))
    g = lax.all_to_all(after(g_parts, *stats[1:]), "blk", 0, 0).reshape(PARTS, (CHUNKS - 1) * PIECE, LANES)
    sides = after(item_sides, g_parts)
    f6, g6, ft3, gt3, w1c, w2c, w1t, w2t = prepare(table(sides, item_modes), spec_w1, spec_w2)
    far = lax.all_gather(after(share, moment), "dp", axis=0)
    mlp_w1, mlp_w2, _ = lax.optimization_barrier((mlp_w1, mlp_w2, stats[3]))
    one = [mlp_w1, swap(mlp_w1, "blk", PARTS, 1)]
    two = [mlp_w2, swap(mlp_w2, "blk", PARTS, 1)]

    b, xn, xhat, r = first_stage(item_sides, after(x, g_parts), stats, gain1, bias1, f6)
    bre, bim, a, p, o = mix_forward(
        b, g6, w1c, spec_b1.reshape(1, 256), w2c, spec_b2.reshape(1, 256), gt3
    )
    far = after(far, bre)
    far = [far, swap(far, "blk", PARTS, 1)]
    first_pieces, x1 = last_stage(own, bre, bim, xn, ft3, None, 0)
    x1_first = [piece.reshape(PIECE, LANES) for piece in exchange(first_pieces)]
    weights = split_weights(own, one, two, far)
    field = after(xn, g, *weights)
    pieces, x1 = last_stage(own, bre, bim, field, ft3, x1, 1)
    x1_later = [piece.reshape((CHUNKS - 1) * PIECE, LANES) for piece in exchange(pieces)]

    x1_first[0] = after(x1_first[0], x1)
    keep, b1s, norms, dx_early = None, [], [], []
    for chunk in range(CHUNKS - 1):
        results = feed(own, x1_later if chunk else x1_first, g, weights, stats, keep, chunk)
        keep = results[:7]
        dx_early.append(exchange(results[7:11]))
        if chunk == 0:
            g_late = lax.all_to_all(after(g_late, results[7]), "blk", 0, 0).reshape(PARTS, PIECE, LANES)
        b1s.append(results[11])
        norms.append(results[12])
    x1_now = [after(x1_later[0], g_late), *x1_later[1:]]
    results = feed_forward(own, x1_now, weights, stats, keep[:4], CHUNKS - 1)
    hh, hl, nh, nl, tip = results[:5]
    branch = lax.all_to_all(after(keep[4], hh), "blk", 0, 0)
    send2, held2 = weight_grads(own, place, dp_size, [after(g, *dx_early[0][1:], *dx_early[1][1:]), g_late], hh, hl, 20)
    local = list(results[5:])
    local[1] = after(local[1], held2)
    results = feed_backward(own, g_late, weights, local, stats, keep[5:7], CHUNKS - 1)
    ph, plo = results[:2]
    b1s.append(results[6])
    norms.append(results[7])
    got2 = after(held2, ph) + swap(send2, "blk", PARTS, 1)
    dx_all = dx_early + [exchange(results[2:6])]
    dx_all = [v.reshape(SLABS, SMAX, LANES) for group in dx_all for v in group]
    tip = lax.all_to_all(after(tip, ph), "blk", 0, 0)
    ph = after(ph, got2, branch)
    send1, held1 = weight_grads(own, place, dp_size, [nh, nl], ph, plo, 20)

    half, cut = dp_size // 2, send1.shape[2] // 2
    mine2 = got2[:, :half] + swap(got2[:, half:], "dp", dp_size, 1)
    got1 = after(held1, *dx_all[-3:]) + swap(send1, "blk", PARTS, 1)
    dx_all[0] = after(dx_all[0], mine2, tip)
    d, dx = first_back(own, dx_all, f6)
    mine2 = after(mine2[0], d) + swap(mine2[1], "blk", PARTS, 2)
    block_output = output_stage(
        item_sides,
        after(x1, d),
        branch.reshape(PARTS, CHUNKS - 1, SLABS, SMAX, LANES),
        tip.reshape(PARTS, SLABS, SMAX, LANES),
        mlp_b2.reshape(1, LANES),
    )
    early = mix_backward(after(d, got1, mine2, block_output), a, p, o, g6, w1t, w2t, gt3, None, None)
    kept = after(got1, early[0])
    one = kept[:, :half, :cut] + swap(got1[:, half:, :cut], "dp", dp_size, 1)
    two = kept[0, :, cut:] + swap(got1[1, :, cut:], "blk", PARTS, 2)
    second = scatter_last(after(mine2, d), dp_size, early[0])
    d_late = after(d, early[0], second, one, two)
    late = mix_backward(d_late, a, p, o, g6, w1t, w2t, gt3, early[2:], grad_b2)
    near2 = gather_near(after(second, early[0]), dp_size, late[0])
    one = after(one[0], late[0]) + swap(one[1], "blk", PARTS, 2)
    two = after(two[:half], late[0]) + swap(two[half:], "dp", dp_size, 1)
    quarters = [early[0], late[0], early[1], late[1]]
    dx_gated = after(dx, near2, one, two)
    dn, pack, *sums = last_back(quarters, dx_gated, xhat, gain1, ft3, late[2], b1s, norms)
    first = scatter_last(jnp.concatenate([one, two], axis=1), dp_size, dn)
    far2 = swap(after(near2, late[0]), "dp", dp_size, 1)
    sums = exchange([after(value, first) for value in sums])
    input_grad = final_stage(item_sides, after(dx, far2), dn, xhat, sums, r, gain1)
    tail = sums[0][-1] + sums[1][-1] + sums[2][-1] + sums[3][-1]
    pack = jnp.concatenate([pack, tail], axis=0)
    near1 = gather_near(first, dp_size, input_grad)
    pack = after(pack, input_grad) + swap(pack, "dp", dp_size, 1)
    distance = 2
    while distance < dp_size:
        pack = pack + swap(pack, "dp", dp_size, distance)
        distance *= 2
    far1 = swap(near1, "dp", dp_size, 1)
    w1_grad = assemble(place, near1, far1, False)
    w2_grad = assemble(place, near2, far2, True)

    spec = pack[: 4 * FREQ].reshape(2, 2, FREQ, 2, FREQ).transpose(0, 1, 3, 2, 4)
    rest = pack[4 * FREQ :]
    return (
        block_output.reshape(SMAX * SMAX, LANES),
        input_grad.reshape(SMAX * SMAX, LANES),
        rest[5],
        rest[6],
        spec[0],
        rest[0:2].reshape(2, 2, 64),
        spec[1],
        rest[2:4].reshape(2, 2, 64),
        rest[12],
        rest[13],
        w1_grad,
        rest[8:12].reshape(HID),
        w2_grad,
        rest[4],
    )


def solution(mesh):
    in_specs = (
        P("dp", "blk"),
        P("dp", "blk"),
        P("dp"),
        P("dp"),
        P("blk"),
        P("blk"),
        P(None, "blk", None, None),
        P(None, "blk", None),
        P(None, "blk", None, None),
        P(None, "blk", None),
        P("blk"),
        P("blk"),
        P(None, "blk"),
        P("blk"),
        P("blk", None),
        P("blk"),
    )
    out_specs = (
        P("dp", "blk"),
        P("dp", "blk"),
        P("blk"),
        P("blk"),
        P(None, "blk", None, None),
        P(None, "blk", None),
        P(None, "blk", None, None),
        P(None, "blk", None),
        P("blk"),
        P("blk"),
        P(None, "blk"),
        P("blk"),
        P("blk", None),
        P("blk"),
    )
    return jax.shard_map(
        functools.partial(per_device, mesh.shape["dp"]),
        mesh=mesh,
        in_specs=in_specs,
        out_specs=out_specs,
        check_vma=False,
    )
```

profile of v0, /device:TPU:0, one launch (start us, length us, event | category | flops | bytes accessed | tf_op | source)
XLA Modules:
  0.0 377.2 jit_solution(11584152330664294462)
XLA Ops:
  8.3 3.0 collective-permute-start.4
  11.9 4.9 %shard_map.263.refs_0_.refs_10_.refs_9_ = f32[25,8,128]{2,1,0:T(8,128)} custom-call(s32[1]{0:T(128)} %copy.62.side_ref, f32[96,96,128]{2,1,0:T(8,128)} %bitcast.120, f32[4,128]{1,0:T(4,128)} %bitcast.135, f32[1,128]{1,0:T(1,128)} %bitcast.136, f32[1,128]{1,0:T(1,128)} %bitcast.137), custom_call_target="tpu_custom_call" | custom-call | flops 6000000000 | bytes 18000000 | tf_op jit(solution)/shard_map/pallas_call | solution.py:226
  21.0 1.7 multiply_select_fusion.f_ref
  22.7 5.6 %shard_map.264 = (f32[4,2,8,96,128]{4,3,2,1,0:T(8,128)}, f32[4,1,8,96,128]{4,3,2,1,0:T(8,128)}, f32[8,128]{1,0:T(8,128)}) custom-call(s32[1]{0:T(128)} %copy.62.side_ref, f32[96,96,128]{2,1,0:T(8,128)} %bitcast.119), custom_call_target="tpu_custom_call" | custom-call | flops 5000000000 | bytes 15000000 | tf_op jit(solution)/shard_map/pallas_call | solution.py:271
  28.3 3.0 shard_map.265
  32.6 4.9 %all-to-all-start = ((f32[4,2,8,96,128]{4,3,2,1,0:T(8,128)}), f32[4,2,8,96,128]{4,3,2,1,0:T(8,128)}, u32[]{:S(2)}, u32[]{:S(2)}) async-start(f32[4,2,8,96,128]{4,3,2,1,0:T(8,128)} %get-tuple-element.165), calls=%async_computation | async-start | bytes 6291456 | tf_op jit(solution)/shard_map/all_to_all | solution.py:1145
  37.5 10.3 %shard_map.266 = (f32[96,64,128]{2,1,0:T(8,128)}, f32[96,96,128]{2,1,0:T(8,128)}, f32[96,96,128]{2,1,0:T(8,128)}, f32[96,128]{1,0:T(8,128)}) custom-call(s32[1]{0:T(128)} %copy.62.side_ref, f32[96,96,128]{2,1,0:T(8,128)} %bitcast.121, f32[25,8,128]{2,1,0:T(8,128)} %shard_map.263.refs_0_.refs_10_.refs_9_, f32[25,8,128]{2,1,0:T(8,128)} %copy-done.25, ...), custom_call_target="tpu_custom_call" | custom-call | flops 3000000000 | bytes 9000000 | tf_op jit(solution)/shard_map/pallas_call | solution.py:325
  47.9 22.3 %shard_map.267 = (f32[96,32,128]{2,1,0:T(8,128)}, f32[96,32,128]{2,1,0:T(8,128)}, f32[4096,256]{1,0:T(8,128)}, f32[4096,256]{1,0:T(8,128)}, f32[4096,256]{1,0:T(8,128)}) custom-call(f32[96,64,128]{2,1,0:T(8,128)} %get-tuple-element.157.re_ref.im_ref, f32[96,64,128]{2,1,0:T(8,128)} %get-tuple-element.157.re_ref.im_ref, ...), custom_call_target="tpu_custom_call" | custom-call | flops 100000000 | bytes 300000 | tf_op jit(solution)/shard_map/pallas_call | solution.py:419
  71.3 3.6 shard_map.269
  74.9 1.9 collective-permute-start.8
  77.5 1.8 collective-permute-start.9
  80.6 7.3 %shard_map.268 = (bf16[4,512,512]{2,1,0:T(8,128)(2,1)}, bf16[4,512,512]{2,1,0:T(8,128)(2,1)}, bf16[4,512,512]{2,1,0:T(8,128)(2,1)}, bf16[4,512,512]{2,1,0:T(8,128)(2,1)}) custom-call(s32[1]{0:T(128)} %bitcast.own_ref.refs_0_, f32[512,512]{1,0:T(8,128)} %refs_0_, f32[512,512]{1,0:T(8,128)} %collective-permute-done.3.refs_1_, f32[8,2,64,512]{3,2,1,0:T(8,128)} %bitcast.106, ...), custom_call_target="tpu_custom_call" | custom-call | flops 100000000 | bytes 300000 | tf_op jit(solution)/shard_map/pallas_call | solution.py:505
  87.9 5.0 %shard_map.270 = (f32[2,8,96,128]{3,2,1,0:T(8,128)}, f32[2,8,96,128]{3,2,1,0:T(8,128)}, f32[2,8,96,128]{3,2,1,0:T(8,128)}, f32[2,8,96,128]{3,2,1,0:T(8,128)}, f32[96,96,128]{2,1,0:T(8,128)}) custom-call(s32[1]{0:T(128)} %bitcast.own_ref.refs_0_, f32[96,32,128]{2,1,0:T(8,128)} %get-tuple-element.162.re_ref, ...), custom_call_target="tpu_custom_call", output_to_operand_aliasing={{4}: (5, {})} | custom-call | flops 200000000 | bytes 600000 | tf_op jit(solution)/shard_map/pallas_call | solution.py:470
  94.9 28.5 %shard_map.271 = (bf16[2304,2048]{1,0:T(8,128)(2,1)}, bf16[2304,2048]{1,0:T(8,128)(2,1)}, bf16[2304,512]{1,0:T(8,128)(2,1)}, bf16[2304,512]{1,0:T(8,128)(2,1)}, ...) custom-call(s32[1]{0:T(128)} %bitcast.own_ref.refs_0_, ...), custom_call_target="tpu_custom_call" | custom-call | flops 28000000000 | bytes 84000000 | tf_op jit(solution)/shard_map/pallas_call | solution.py:735
  123.4 3.8 %all-to-all-start.1 = ((f32[4,1,8,96,128]{4,3,2,1,0:T(8,128)}), f32[4,1,8,96,128]{4,3,2,1,0:T(8,128)S(1)}, u32[]{:S(2)}, u32[]{:S(2)}) async-start(f32[4,1,8,96,128]{4,3,2,1,0:T(8,128)} %get-tuple-element.186), calls=%async_computation.1 | async-start | bytes 3145728 | tf_op jit(solution)/shard_map/all_to_all | solution.py:1173
  127.7 1.7 collective-permute-start.14
  130.6 28.5 %shard_map.272 = (bf16[2304,2048]{1,0:T(8,128)(2,1)}, bf16[2304,2048]{1,0:T(8,128)(2,1)}, bf16[2304,512]{1,0:T(8,128)(2,1)}, bf16[2304,512]{1,0:T(8,128)(2,1)}, ...) custom-call(s32[1]{0:T(128)} %bitcast.own_ref.refs_0_, ...), custom_call_target="tpu_custom_call", output_to_operand_aliasing={{0}: (14, {}), {1}: (15, {}), {2}: (16, {}), {3}: (17, {}),... | custom-call | flops 28000000000 | bytes 84000000 | tf_op jit(solution)/shard_map/pallas_call | solution.py:735
  159.4 1.7 collective-permute-start.17
  161.2 19.7 %shard_map.273 = (bf16[2304,2048]{1,0:T(8,128)(2,1)}, bf16[2304,2048]{1,0:T(8,128)(2,1)}, bf16[2304,512]{1,0:T(8,128)(2,1)}, bf16[2304,512]{1,0:T(8,128)(2,1)}, ...) custom-call(s32[1]{0:T(128)} %bitcast.own_ref.refs_0_, ...), custom_call_target="tpu_custom_call", output_to_operand_aliasing={{0}: (13, {}), {1}: (14, {}), {2}: (15, {}), {3}: (16, {})} | custom-call | flops 17999998976 | bytes 54000000 | tf_op jit(solution)/shard_map/pallas_call | solution.py:735
  180.9 4.7 %all-to-all-start.3 = ((f32[4,2,768,128]{3,2,1,0:T(8,128)}), f32[4,2,768,128]{3,2,1,0:T(8,128)}, u32[]{:S(2)}, u32[]{:S(2)}) async-start(f32[4,2,768,128]{3,2,1,0:T(8,128)} %get-tuple-element.232), calls=%async_computation.3 | async-start | bytes 6291456 | tf_op jit(solution)/shard_map/all_to_all | solution.py:1179
  185.7 22.4 %shard_map.274 = (f32[2,8,64,512]{3,2,1,0:T(8,128)}, f32[2,8,64,512]{3,2,1,0:T(8,128)}) custom-call(s32[1]{0:T(128)} %bitcast.own_ref.refs_0_, s32[1]{0:T(128)} %bitcast.19.place_ref, bf16[2304,2048]{1,0:T(8,128)(2,1)} %get-tuple-element.202.th, bf16[2304,2048]{1,0:T(8,128)(2,1)} %get-tuple-element.203.tl, f32[4,1536,128]{2,1,0:T(8,128)} %bitcast.10.refs_5_.refs_0_, ...), custom_call_target="tpu_custom_call" | custom-call | flops 20000000000 | bytes 60000000 | tf_op jit(solution)/shard_map/pallas_call | solution.py:802
  208.6 17.1 %shard_map.275 = (bf16[2304,2048]{1,0:T(8,128)(2,1)}, bf16[2304,2048]{1,0:T(8,128)(2,1)}, f32[768,128]{1,0:T(8,128)}, f32[768,128]{1,0:T(8,128)}, f32[768,128]{1...) custom-call(s32[1]{0:T(128)} %bitcast.own_ref.refs_0_, ...), custom_call_target="tpu_custom_call", output_to_operand_aliasing={{0}: (13, {}), {1}: (14, {})} | custom-call | flops 16000000000 | bytes 48000000 | tf_op jit(solution)/shard_map/pallas_call | solution.py:735
  225.9 2.0 collective-permute-start.22
  228.5 1.8 collective-permute-start.20
  230.3 4.7 %all-to-all-start.2 = ((f32[4,1,768,128]{3,2,1,0:T(8,128)}), f32[4,1,768,128]{3,2,1,0:T(8,128)}, u32[]{:S(2)}, u32[]{:S(2)}) async-start(f32[4,1,768,128]{3,2,1,0:T(8,128)} %get-tuple-element.222), calls=%async_computation.2 | async-start | bytes 3145728 | tf_op jit(solution)/shard_map/all_to_all | solution.py:1190
  235.1 22.1 %shard_map.278 = (f32[2,8,64,512]{3,2,1,0:T(8,128)}, f32[2,8,64,512]{3,2,1,0:T(8,128)}) custom-call(s32[1]{0:T(128)} %bitcast.own_ref.refs_0_, s32[1]{0:T(128)} %bitcast.19.place_ref, bf16[2304,2048]{1,0:T(8,128)(2,1)} %get-tuple-element.236.th, bf16[2304,2048]{1,0:T(8,128)(2,1)} %get-tuple-element.237.tl, bf16[2304,512]{1,0:T(8,128)(2,1)} %get-tuple-element.238.refs_0_, ...), custom_call_target="tpu_custom_call" | custom-call | flops 20000000000 | bytes 60000000 | tf_op jit(solution)/shard_map/pallas_call | solution.py:802
  259.2 3.7 all-to-all-done.2
  263.1 1.7 collective-permute-start.24
  264.8 6.8 %shard_map.276 = (f32[96,64,128]{2,1,0:T(8,128)}, f32[96,96,128]{2,1,0:T(8,128)}) custom-call(s32[1]{0:T(128)} %bitcast.own_ref.refs_0_, bf16[64,768]{1,0:T(8,128)(2,1)} %get-tuple-element.156.refs_6_.f6_ref, f32[8,96,128]{2,1,0:T(8,128)} %bitcast.145, f32[8,96,128]{2,1,0:T(8,128)} %bitcast.128, f32[8,96,128]{2,1,0:T(8,128)} %bitcast.26.refs_2_, ...), custom_call_target="tpu_custom_call" | custom-call | flops 8000000000 | bytes 24000000 | tf_op jit(solution)/shard_map/pallas_call | solution.py:858
  271.6 6.5 %shard_map.277 = f32[96,96,128]{2,1,0:T(8,128)} custom-call(s32[1]{0:T(128)} %copy.62.side_ref, f32[96,96,128]{2,1,0:T(8,128)} %get-tuple-element.230.x_ref, f32[4,2,8,96,128]{4,3,2,1,0:T(8,128)} %bitcast.36.y_ref, f32[4,8,96,128]{3,2,1,0:T(8,128)} %bitcast.37.tip_ref, f32[1,128]{1,0:T(1,128)} %bitcast.139), custom_call_target="tpu_custom_call" | custom-call | flops 5000000000 | bytes 15000000 | tf_op jit(solution)/shard_map/pallas_call | solution.py:1066
  278.2 1.9 collective-permute-start.26
  280.1 2.5 collective-permute-start.28
  282.7 2.1 add.93
  286.8 10.1 %shard_map.279 = (f32[96,16,128]{2,1,0:T(8,128)}, f32[96,16,128]{2,1,0:T(8,128)}, f32[256,256]{1,0:T(8,128)}, f32[256,256]{1,0:T(8,128)}, f32[8,256]{1,0:T(8,128)}, /*index=5*/f32[8,256]{1,0:T(8,128)}) custom-call(f32[96,64,128]{2,1,0:T(8,128)} %get-tuple-element.253.refs_0_.refs_1_, f32[96,64,128]{2,1,0:T(8,128)} %get-tuple-element.253.refs_0_.refs_1_, ...), custom_call_target="tpu_custom_call" | custom-call | flops 12999999488 | bytes 39000000 | tf_op jit(solution)/shard_map/pallas_call | solution.py:950
  296.9 3.0 collective-permute-start.33
  301.6 1.7 collective-permute-start.35
  303.9 10.5 %shard_map.280 = (f32[96,16,128]{2,1,0:T(8,128)}, f32[96,16,128]{2,1,0:T(8,128)}, f32[264,128]{1,0:T(8,128)}) custom-call(f32[96,64,128]{2,1,0:T(8,128)} %get-tuple-element.253.refs_0_.refs_1_, f32[96,64,128]{2,1,0:T(8,128)} %get-tuple-element.253.refs_0_.refs_1_, f32[4096,256]{1,0:T(8,128)} %get-tuple-element.244.refs_2_, ...), custom_call_target="tpu_custom_call" | custom-call | flops 12999999488 | bytes 39000000 | tf_op jit(solution)/shard_map/pallas_call | solution.py:950
  317.2 2.5 collective-permute-start.39
  319.7 9.7 %shard_map.281 = (f32[96,96,128]{2,1,0:T(8,128)}, f32[264,128]{1,0:T(8,128)}, f32[25,8,128]{2,1,0:T(8,128)}, f32[25,8,128]{2,1,0:T(8,128)}, f32[25,8,128]{2,1,0:T(8,128)}, /*index=5*/f32[25,8,128]{2,1,0:T(8,128)}) custom-call(f32[96,16,128]{2,1,0:T(8,128)} %get-tuple-element.249.re0, f32[96,16,128]{2,1,0:T(8,128)} %get-tuple-element.259.re1, ...), custom_call_target="tpu_custom_call" | custom-call | flops 12999999488 | bytes 39000000 | tf_op jit(solution)/shard_map/pallas_call | solution.py:1007
  331.4 2.9 collective-permute-start.48
  335.5 1.9 collective-permute-start.46
  339.6 9.4 %shard_map.282 = f32[96,96,128]{2,1,0:T(8,128)} custom-call(s32[1]{0:T(128)} %copy.62.side_ref, f32[96,96,128]{2,1,0:T(8,128)} %get-tuple-element.267.dx_ref, f32[96,96,128]{2,1,0:T(8,128)} %get-tuple-element.276.dn_ref, f32[96,96,128]{2,1,0:T(8,128)} %get-tuple-element.268.xhat_ref, f32[96,128]{1,0:T(8,128)} %get-tuple-element.277.r_ref, ...), custom_call_target="tpu_custom_call" | custom-call | flops 12999999488 | bytes 39000000 | tf_op jit(solution)/shard_map/pallas_call | solution.py:1042
  350.5 1.6 collective-permute-start.49
  352.1 2.5 collective-permute-done.44
  354.6 2.8 collective-permute-start.45
  357.4 2.6 shard_map.284
  360.0 3.7 collective-permute-done.45
  367.9 2.2 shard_map.283
  (179 shorter events, 34.8 us)
Async XLA Ops:
  7.2 63.0 %all-gather.3.cloned.1.call-start = ((), (), s32[]{:S(2)}) async-start(), calls=%async_computation.4 | async-start | bytes 2359296 | tf_op jit(solution)/shard_map/all_gather | solution.py:1148
  8.3 9.3 %collective-permute-start.4 = (f32[2,64,512]{2,1,0:T(8,128)S(1)}, f32[2,64,512]{2,1,0:T(8,128)S(1)}, u32[]{:S(2)}, u32[]{:S(2)}) collective-permute-start(f32[2,64,512]{2,1,0:T(8,128)S(1)} %pad_maximum_fusion.2), channel_id=1, source_target_pairs={{0,2},{1,3},{2,0},{3,1},{4,6},{5,7},{6,4},{7,5},{8,10},{9,11},{10,... | collective-permute-start | bytes 786440 | tf_op jit(solution)/shard_map/ppermute | solution.py:1085
  18.3 14.3 %collective-permute-start.2 = (f32[25,8,128]{2,1,0:T(8,128)}, f32[25,8,128]{2,1,0:T(8,128)S(1)}, u32[]{:S(2)}, u32[]{:S(2)}) collective-permute-start(f32[25,8,128]{2,1,0:T(8,128)} %shard_map.263.refs_0_.refs_10_.refs_9_), channel_id=1, source_target_pairs={{0,3},{1,2},{2,1},{3,0},{4,7},{5,6},{6,5},{7,4},{8,11},{9,10},{10,... | collective-permute-start | bytes 307208 | tf_op jit(solution)/shard_map/ppermute | solution.py:1085
  18.7 13.9 %collective-permute-start.1 = (f32[25,8,128]{2,1,0:T(8,128)}, f32[25,8,128]{2,1,0:T(8,128)S(1)}, u32[]{:S(2)}, u32[]{:S(2)}) collective-permute-start(f32[25,8,128]{2,1,0:T(8,128)} %shard_map.263.refs_0_.refs_10_.refs_9_), channel_id=1, source_target_pairs={{0,2},{1,3},{2,0},{3,1},{4,6},{5,7},{6,4},{7,5},{8,10},{9,11},{10,... | collective-permute-start | bytes 307208 | tf_op jit(solution)/shard_map/ppermute | solution.py:1085
  20.2 12.4 %collective-permute-start = (f32[25,8,128]{2,1,0:T(8,128)}, f32[25,8,128]{2,1,0:T(8,128)S(1)}, u32[]{:S(2)}, u32[]{:S(2)}) collective-permute-start(f32[25,8,128]{2,1,0:T(8,128)} %shard_map.263.refs_0_.refs_10_.refs_9_), channel_id=1, source_target_pairs={{0,1},{1,0},{2,3},{3,2},{4,5},{5,4},{6,7},{7,6},{8,9},{9,8},{10,11... | collective-permute-start | bytes 307208 | tf_op jit(solution)/shard_map/ppermute | solution.py:1085
  32.6 55.3 %all-to-all-start = ((f32[4,2,8,96,128]{4,3,2,1,0:T(8,128)}), f32[4,2,8,96,128]{4,3,2,1,0:T(8,128)}, u32[]{:S(2)}, u32[]{:S(2)}) async-start(f32[4,2,8,96,128]{4,3,2,1,0:T(8,128)} %get-tuple-element.165), calls=%async_computation | async-start | bytes 6291456 | tf_op jit(solution)/shard_map/all_to_all | solution.py:1145
  74.9 19.3 %collective-permute-start.7 = (f32[8,96,128]{2,1,0:T(8,128)}, f32[8,96,128]{2,1,0:T(8,128)S(1)}, u32[]{:S(2)}, u32[]{:S(2)}) collective-permute-start(f32[8,96,128]{2,1,0:T(8,128)} %get-tuple-element.180), channel_id=1, source_target_pairs={{0,1},{1,0},{2,3},{3,2},{4,5},{5,4},{6,7},{7,6},{8,9},{9,8},{10,11... | collective-permute-start | bytes 1179656 | tf_op jit(solution)/shard_map/ppermute | solution.py:1085
  74.9 19.9 %collective-permute-start.8 = (f32[8,96,128]{2,1,0:T(8,128)}, f32[8,96,128]{2,1,0:T(8,128)}, u32[]{:S(2)}, u32[]{:S(2)}) collective-permute-start(f32[8,96,128]{2,1,0:T(8,128)} %get-tuple-element.181), channel_id=1, source_target_pairs={{0,2},{1,3},{2,0},{3,1},{4,6},{5,7},{6,4},{7,5},{8,10},{9,11},{10,... | collective-permute-start | bytes 1179656 | tf_op jit(solution)/shard_map/ppermute | solution.py:1085
  77.5 17.3 %collective-permute-start.9 = (f32[8,96,128]{2,1,0:T(8,128)}, f32[8,96,128]{2,1,0:T(8,128)}, u32[]{:S(2)}, u32[]{:S(2)}) collective-permute-start(f32[8,96,128]{2,1,0:T(8,128)} %get-tuple-element.182), channel_id=1, source_target_pairs={{0,3},{1,2},{2,1},{3,0},{4,7},{5,6},{6,5},{7,4},{8,11},{9,10},{10,... | collective-permute-start | bytes 1179656 | tf_op jit(solution)/shard_map/ppermute | solution.py:1085
  92.9 36.5 %collective-permute-start.10 = (f32[2,8,96,128]{3,2,1,0:T(8,128)}, f32[2,8,96,128]{3,2,1,0:T(8,128)S(1)}, u32[]{:S(2)}, u32[]{:S(2)}) collective-permute-start(f32[2,8,96,128]{3,2,1,0:T(8,128)} %get-tuple-element.188), channel_id=1, source_target_pairs={{0,1},{1,0},{2,3},{3,2},{4,5},{5,4},{6,7},{7,6},{8,9},{9,8},{10,11... | collective-permute-start | bytes 2359304 | tf_op jit(solution)/shard_map/ppermute | solution.py:1085
  93.1 36.3 %collective-permute-start.11 = (f32[2,8,96,128]{3,2,1,0:T(8,128)}, f32[2,8,96,128]{3,2,1,0:T(8,128)S(1)}, u32[]{:S(2)}, u32[]{:S(2)}) collective-permute-start(f32[2,8,96,128]{3,2,1,0:T(8,128)} %get-tuple-element.189), channel_id=1, source_target_pairs={{0,2},{1,3},{2,0},{3,1},{4,6},{5,7},{6,4},{7,5},{8,10},{9,11},{10,... | collective-permute-start | bytes 2359304 | tf_op jit(solution)/shard_map/ppermute | solution.py:1085
  94.1 35.4 %collective-permute-start.12 = (f32[2,8,96,128]{3,2,1,0:T(8,128)}, f32[2,8,96,128]{3,2,1,0:T(8,128)}, u32[]{:S(2)}, u32[]{:S(2)}) collective-permute-start(f32[2,8,96,128]{3,2,1,0:T(8,128)} %get-tuple-element.190), channel_id=1, source_target_pairs={{0,3},{1,2},{2,1},{3,0},{4,7},{5,6},{6,5},{7,4},{8,11},{9,10},{10,... | collective-permute-start | bytes 2359304 | tf_op jit(solution)/shard_map/ppermute | solution.py:1085
  123.4 37.7 %all-to-all-start.1 = ((f32[4,1,8,96,128]{4,3,2,1,0:T(8,128)}), f32[4,1,8,96,128]{4,3,2,1,0:T(8,128)S(1)}, u32[]{:S(2)}, u32[]{:S(2)}) async-start(f32[4,1,8,96,128]{4,3,2,1,0:T(8,128)} %get-tuple-element.186), calls=%async_computation.1 | async-start | bytes 3145728 | tf_op jit(solution)/shard_map/all_to_all | solution.py:1173
  127.2 33.9 %collective-permute-start.13 = (f32[768,128]{1,0:T(8,128)}, f32[768,128]{1,0:T(8,128)S(1)}, u32[]{:S(2)}, u32[]{:S(2)}) collective-permute-start(f32[768,128]{1,0:T(8,128)} %get-tuple-element.204), channel_id=1, source_target_pairs={{0,1},{1,0},{2,3},{3,2},{4,5},{5,4},{6,7},{7,6},{8,9},{9,8},{10,11... | collective-permute-start | bytes 1179656 | tf_op jit(solution)/shard_map/ppermute | solution.py:1085
  127.7 57.9 %collective-permute-start.14 = (f32[768,128]{1,0:T(8,128)}, f32[768,128]{1,0:T(8,128)}, u32[]{:S(2)}, u32[]{:S(2)}) collective-permute-start(f32[768,128]{1,0:T(8,128)} %get-tuple-element.205), channel_id=1, source_target_pairs={{0,2},{1,3},{2,0},{3,1},{4,6},{5,7},{6,4},{7,5},{8,10},{9,11},{10,... | collective-permute-start | bytes 1179656 | tf_op jit(solution)/shard_map/ppermute | solution.py:1085
  129.4 56.2 %collective-permute-start.15 = (f32[768,128]{1,0:T(8,128)}, f32[768,128]{1,0:T(8,128)}, u32[]{:S(2)}, u32[]{:S(2)}) collective-permute-start(f32[768,128]{1,0:T(8,128)} %get-tuple-element.206), channel_id=1, source_target_pairs={{0,3},{1,2},{2,1},{3,0},{4,7},{5,6},{6,5},{7,4},{8,11},{9,10},{10,... | collective-permute-start | bytes 1179656 | tf_op jit(solution)/shard_map/ppermute | solution.py:1085
  159.1 26.5 %collective-permute-start.16 = (f32[768,128]{1,0:T(8,128)}, f32[768,128]{1,0:T(8,128)S(1)}, u32[]{:S(2)}, u32[]{:S(2)}) collective-permute-start(f32[768,128]{1,0:T(8,128)} %get-tuple-element.207), channel_id=1, source_target_pairs={{0,1},{1,0},{2,3},{3,2},{4,5},{5,4},{6,7},{7,6},{8,9},{9,8},{10,11... | collective-permute-start | bytes 1179656 | tf_op jit(solution)/shard_map/ppermute | solution.py:1085
  159.4 26.3 %collective-permute-start.17 = (f32[768,128]{1,0:T(8,128)}, f32[768,128]{1,0:T(8,128)S(1)}, u32[]{:S(2)}, u32[]{:S(2)}) collective-permute-start(f32[768,128]{1,0:T(8,128)} %get-tuple-element.208), channel_id=1, source_target_pairs={{0,2},{1,3},{2,0},{3,1},{4,6},{5,7},{6,4},{7,5},{8,10},{9,11},{10,... | collective-permute-start | bytes 1179656 | tf_op jit(solution)/shard_map/ppermute | solution.py:1085
  161.1 24.6 %collective-permute-start.18 = (f32[768,128]{1,0:T(8,128)}, f32[768,128]{1,0:T(8,128)S(1)}, u32[]{:S(2)}, u32[]{:S(2)}) collective-permute-start(f32[768,128]{1,0:T(8,128)} %get-tuple-element.209), channel_id=1, source_target_pairs={{0,3},{1,2},{2,1},{3,0},{4,7},{5,6},{6,5},{7,4},{8,11},{9,10},{10,... | collective-permute-start | bytes 1179656 | tf_op jit(solution)/shard_map/ppermute | solution.py:1085
  180.9 49.4 %all-to-all-start.3 = ((f32[4,2,768,128]{3,2,1,0:T(8,128)}), f32[4,2,768,128]{3,2,1,0:T(8,128)}, u32[]{:S(2)}, u32[]{:S(2)}) async-start(f32[4,2,768,128]{3,2,1,0:T(8,128)} %get-tuple-element.232), calls=%async_computation.3 | async-start | bytes 6291456 | tf_op jit(solution)/shard_map/all_to_all | solution.py:1179
  208.1 19.7 %collective-permute-start.19 = (f32[2,8,64,512]{3,2,1,0:T(8,128)}, f32[2,8,64,512]{3,2,1,0:T(8,128)S(1)}, u32[]{:S(2)}, u32[]{:S(2)}) collective-permute-start(f32[2,8,64,512]{3,2,1,0:T(8,128)} %get-tuple-element.220), channel_id=1, source_target_pairs={{0,1},{1,0},{2,3},{3,2},{4,5},{5,4},{6,7},{7,6},{8,9},{9,8},{10,11... | collective-permute-start | bytes 6291464 | tf_op jit(solution)/shard_map/ppermute | solution.py:1085
  225.8 31.9 %collective-permute-start.21 = (f32[768,128]{1,0:T(8,128)}, f32[768,128]{1,0:T(8,128)S(1)}, u32[]{:S(2)}, u32[]{:S(2)}) collective-permute-start(f32[768,128]{1,0:T(8,128)} %get-tuple-element.226), channel_id=1, source_target_pairs={{0,1},{1,0},{2,3},{3,2},{4,5},{5,4},{6,7},{7,6},{8,9},{9,8},{10,11... | collective-permute-start | bytes 1179656 | tf_op jit(solution)/shard_map/ppermute | solution.py:1085
  225.9 31.7 %collective-permute-start.22 = (f32[768,128]{1,0:T(8,128)}, f32[768,128]{1,0:T(8,128)}, u32[]{:S(2)}, u32[]{:S(2)}) collective-permute-start(f32[768,128]{1,0:T(8,128)} %get-tuple-element.227), channel_id=1, source_target_pairs={{0,2},{1,3},{2,0},{3,1},{4,6},{5,7},{6,4},{7,5},{8,10},{9,11},{10,... | collective-permute-start | bytes 1179656 | tf_op jit(solution)/shard_map/ppermute | solution.py:1085
  227.9 29.8 %collective-permute-start.23 = (f32[768,128]{1,0:T(8,128)}, f32[768,128]{1,0:T(8,128)}, u32[]{:S(2)}, u32[]{:S(2)}) collective-permute-start(f32[768,128]{1,0:T(8,128)} %get-tuple-element.228), channel_id=1, source_target_pairs={{0,3},{1,2},{2,1},{3,0},{4,7},{5,6},{6,5},{7,4},{8,11},{9,10},{10,... | collective-permute-start | bytes 1179656 | tf_op jit(solution)/shard_map/ppermute | solution.py:1085
  228.5 29.1 %collective-permute-start.20 = (f32[2,4,64,512]{3,2,1,0:T(8,128)S(1)}, f32[2,4,64,512]{3,2,1,0:T(8,128)}, u32[]{:S(2)}, u32[]{:S(2)}) collective-permute-start(f32[2,4,64,512]{3,2,1,0:T(8,128)S(1)} %slice.150), channel_id=1, source_target_pairs={{0,4},{4,0},{8,12},{12,8},{16,20},{20,16},{24,28},{28,24},{1,5},{5... | collective-permute-start | bytes 3145736 | tf_op jit(solution)/shard_map/ppermute | solution.py:1085
  230.3 32.7 %all-to-all-start.2 = ((f32[4,1,768,128]{3,2,1,0:T(8,128)}), f32[4,1,768,128]{3,2,1,0:T(8,128)}, u32[]{:S(2)}, u32[]{:S(2)}) async-start(f32[4,1,768,128]{3,2,1,0:T(8,128)} %get-tuple-element.222), calls=%async_computation.2 | async-start | bytes 3145728 | tf_op jit(solution)/shard_map/all_to_all | solution.py:1190
  257.2 25.5 %collective-permute-start.25 = (f32[2,8,64,512]{3,2,1,0:T(8,128)}, f32[2,8,64,512]{3,2,1,0:T(8,128)}, u32[]{:S(2)}, u32[]{:S(2)}) collective-permute-start(f32[2,8,64,512]{3,2,1,0:T(8,128)} %get-tuple-element.242), channel_id=1, source_target_pairs={{0,1},{1,0},{2,3},{3,2},{4,5},{5,4},{6,7},{7,6},{8,9},{9,8},{10,11... | collective-permute-start | bytes 6291464 | tf_op jit(solution)/shard_map/ppermute | solution.py:1085
  263.1 15.0 %collective-permute-start.24 = (f32[4,64,512]{2,1,0:T(8,128)S(1)}, f32[4,64,512]{2,1,0:T(8,128)S(1)}, u32[]{:S(2)}, u32[]{:S(2)}) collective-permute-start(f32[4,64,512]{2,1,0:T(8,128)S(1)} %get-tuple-element.290), channel_id=1, source_target_pairs={{0,2},{1,3},{2,0},{3,1},{4,6},{5,7},{6,4},{7,5},{8,10},{9,11},{10,... | collective-permute-start | bytes 1572872 | tf_op jit(solution)/shard_map/ppermute | solution.py:1085
  278.2 18.6 %collective-permute-start.26 = (f32[64,512]{1,0:T(8,128)S(1)}, f32[64,512]{1,0:T(8,128)S(1)}, u32[]{:S(2)}, u32[]{:S(2)}) collective-permute-start(f32[64,512]{1,0:T(8,128)S(1)} %get-tuple-element.300), channel_id=1, source_target_pairs={{0,8},{4,12},{8,0},{12,4},{16,24},{20,28},{24,16},{28,20},{1,9},{5... | collective-permute-start | bytes 393224 | tf_op jit(solution)/shard_map/ppermute | solution.py:1085
  280.1 16.7 %collective-permute-start.28 = (f32[64,512]{1,0:T(8,128)S(1)}, f32[64,512]{1,0:T(8,128)S(1)}, u32[]{:S(2)}, u32[]{:S(2)}) collective-permute-start(f32[64,512]{1,0:T(8,128)S(1)} %get-tuple-element.301), channel_id=1, source_target_pairs={{0,24},{4,28},{8,16},{12,20},{16,8},{20,12},{24,0},{28,4},{1,25},{... | collective-permute-start | bytes 393224 | tf_op jit(solution)/shard_map/ppermute | solution.py:1085
  282.6 14.2 %collective-permute-start.27 = (f32[64,512]{1,0:T(8,128)S(1)}, f32[64,512]{1,0:T(8,128)S(1)}, u32[]{:S(2)}, u32[]{:S(2)}) collective-permute-start(f32[64,512]{1,0:T(8,128)S(1)} %get-tuple-element.302), channel_id=1, source_target_pairs={{0,16},{4,20},{8,24},{12,28},{16,0},{20,4},{24,8},{28,12},{1,17},{... | collective-permute-start | bytes 393224 | tf_op jit(solution)/shard_map/ppermute | solution.py:1085
  284.8 16.5 %collective-permute-start.29 = (f32[2,4,32,512]{3,2,1,0:T(8,128)S(1)}, f32[2,4,32,512]{3,2,1,0:T(8,128)S(1)}, u32[]{:S(2)}, u32[]{:S(2)}) collective-permute-start(f32[2,4,32,512]{3,2,1,0:T(8,128)S(1)} %slice.153), channel_id=1, source_target_pairs={{0,4},{4,0},{8,12},{12,8},{16,20},{20,16},{24,28},{28,24},{1,5},{5... | collective-permute-start | bytes 1572872 | tf_op jit(solution)/shard_map/ppermute | solution.py:1085
  286.4 15.1 %collective-permute-start.30 = (f32[8,32,512]{2,1,0:T(8,128)S(1)}, f32[8,32,512]{2,1,0:T(8,128)S(1)}, u32[]{:S(2)}, u32[]{:S(2)}) collective-permute-start(f32[8,32,512]{2,1,0:T(8,128)S(1)} %slice_bitcast_fusion), channel_id=1, source_target_pairs={{0,2},{1,3},{2,0},{3,1},{4,6},{5,7},{6,4},{7,5},{8,10},{9,11},{10,... | collective-permute-start | bytes 1572872 | tf_op jit(solution)/shard_map/ppermute | solution.py:1085
  296.9 17.5 %collective-permute-start.33 = (f32[64,512]{1,0:T(8,128)S(1)}, f32[64,512]{1,0:T(8,128)S(1)}, u32[]{:S(2)}, u32[]{:S(2)}) collective-permute-start(f32[64,512]{1,0:T(8,128)S(1)} %add_add_fusion.1), channel_id=1, source_target_pairs={{0,24},{4,28},{8,16},{12,20},{16,8},{20,12},{24,0},{28,4},{1,25},{... | collective-permute-start | bytes 393224 | tf_op jit(solution)/shard_map/ppermute | solution.py:1085
  299.9 14.5 %collective-permute-start.32 = (f32[64,512]{1,0:T(8,128)S(1)}, f32[64,512]{1,0:T(8,128)S(1)}, u32[]{:S(2)}, u32[]{:S(2)}) collective-permute-start(f32[64,512]{1,0:T(8,128)S(1)} %add_add_fusion.1), channel_id=1, source_target_pairs={{0,16},{4,20},{8,24},{12,28},{16,0},{20,4},{24,8},{28,12},{1,17},{... | collective-permute-start | bytes 393224 | tf_op jit(solution)/shard_map/ppermute | solution.py:1085
  300.3 14.1 %collective-permute-start.31 = (f32[64,512]{1,0:T(8,128)S(1)}, f32[64,512]{1,0:T(8,128)S(1)}, u32[]{:S(2)}, u32[]{:S(2)}) collective-permute-start(f32[64,512]{1,0:T(8,128)S(1)} %add_add_fusion.1), channel_id=1, source_target_pairs={{0,8},{4,12},{8,0},{12,4},{16,24},{20,28},{24,16},{28,20},{1,9},{5... | collective-permute-start | bytes 393224 | tf_op jit(solution)/shard_map/ppermute | solution.py:1085
  301.6 14.4 %collective-permute-start.35 = (f32[4,32,512]{2,1,0:T(8,128)S(1)}, f32[4,32,512]{2,1,0:T(8,128)S(1)}, u32[]{:S(2)}, u32[]{:S(2)}) collective-permute-start(f32[4,32,512]{2,1,0:T(8,128)S(1)} %get-tuple-element.298), channel_id=1, source_target_pairs={{0,2},{1,3},{2,0},{3,1},{4,6},{5,7},{6,4},{7,5},{8,10},{9,11},{10,... | collective-permute-start | bytes 786440 | tf_op jit(solution)/shard_map/ppermute | solution.py:1085
  303.3 12.7 %collective-permute-start.36 = (f32[4,32,512]{2,1,0:T(8,128)S(1)}, f32[4,32,512]{2,1,0:T(8,128)S(1)}, u32[]{:S(2)}, u32[]{:S(2)}) collective-permute-start(f32[4,32,512]{2,1,0:T(8,128)S(1)} %get-tuple-element.296), channel_id=1, source_target_pairs={{0,4},{4,0},{8,12},{12,8},{16,20},{20,16},{24,28},{28,24},{1,5},{5... | collective-permute-start | bytes 786440 | tf_op jit(solution)/shard_map/ppermute | solution.py:1085
  314.4 25.1 %collective-permute-start.34 = (f32[4,64,512]{2,1,0:T(8,128)S(1)}, f32[4,64,512]{2,1,0:T(8,128)S(1)}, u32[]{:S(2)}, u32[]{:S(2)}) collective-permute-start(f32[4,64,512]{2,1,0:T(8,128)S(1)} %pad_maximum_fusion.near), channel_id=1, source_target_pairs={{0,4},{4,0},{8,12},{12,8},{16,20},{20,16},{24,28},{28,24},{1,5},{5... | collective-permute-start | bytes 1572872 | tf_op jit(solution)/shard_map/ppermute | solution.py:1085
  316.1 13.3 %collective-permute-start.37 = (f32[64,512]{1,0:T(8,128)S(1)}, f32[64,512]{1,0:T(8,128)S(1)}, u32[]{:S(2)}, u32[]{:S(2)}) collective-permute-start(f32[64,512]{1,0:T(8,128)S(1)} %get-tuple-element.292), channel_id=1, source_target_pairs={{0,8},{4,12},{8,0},{12,4},{16,24},{20,28},{24,16},{28,20},{1,9},{5... | collective-permute-start | bytes 393224 | tf_op jit(solution)/shard_map/ppermute | solution.py:1085
  317.2 12.2 %collective-permute-start.39 = (f32[64,512]{1,0:T(8,128)S(1)}, f32[64,512]{1,0:T(8,128)S(1)}, u32[]{:S(2)}, u32[]{:S(2)}) collective-permute-start(f32[64,512]{1,0:T(8,128)S(1)} %get-tuple-element.294), channel_id=1, source_target_pairs={{0,24},{4,28},{8,16},{12,20},{16,8},{20,12},{24,0},{28,4},{1,25},{... | collective-permute-start | bytes 393224 | tf_op jit(solution)/shard_map/ppermute | solution.py:1085
  319.6 9.8 %collective-permute-start.38 = (f32[64,512]{1,0:T(8,128)S(1)}, f32[64,512]{1,0:T(8,128)S(1)}, u32[]{:S(2)}, u32[]{:S(2)}) collective-permute-start(f32[64,512]{1,0:T(8,128)S(1)} %get-tuple-element.295), channel_id=1, source_target_pairs={{0,16},{4,20},{8,24},{12,28},{16,0},{20,4},{24,8},{28,12},{1,17},{... | collective-permute-start | bytes 393224 | tf_op jit(solution)/shard_map/ppermute | solution.py:1085
  331.4 19.0 %collective-permute-start.48 = (f32[64,512]{1,0:T(8,128)S(1)}, f32[64,512]{1,0:T(8,128)S(1)}, u32[]{:S(2)}, u32[]{:S(2)}) collective-permute-start(f32[64,512]{1,0:T(8,128)S(1)} %add_add_fusion), channel_id=1, source_target_pairs={{0,24},{4,28},{8,16},{12,20},{16,8},{20,12},{24,0},{28,4},{1,25},{... | collective-permute-start | bytes 393224 | tf_op jit(solution)/shard_map/ppermute | solution.py:1085
  334.3 16.1 %collective-permute-start.47 = (f32[64,512]{1,0:T(8,128)S(1)}, f32[64,512]{1,0:T(8,128)S(1)}, u32[]{:S(2)}, u32[]{:S(2)}) collective-permute-start(f32[64,512]{1,0:T(8,128)S(1)} %add_add_fusion), channel_id=1, source_target_pairs={{0,16},{4,20},{8,24},{12,28},{16,0},{20,4},{24,8},{28,12},{1,17},{... | collective-permute-start | bytes 393224 | tf_op jit(solution)/shard_map/ppermute | solution.py:1085
  335.5 14.9 %collective-permute-start.46 = (f32[64,512]{1,0:T(8,128)S(1)}, f32[64,512]{1,0:T(8,128)S(1)}, u32[]{:S(2)}, u32[]{:S(2)}) collective-permute-start(f32[64,512]{1,0:T(8,128)S(1)} %add_add_fusion), channel_id=1, source_target_pairs={{0,8},{4,12},{8,0},{12,4},{16,24},{20,28},{24,16},{28,20},{1,9},{5... | collective-permute-start | bytes 393224 | tf_op jit(solution)/shard_map/ppermute | solution.py:1085
  339.0 10.0 %collective-permute-start.43 = (f32[272,128]{1,0:T(8,128)S(1)}, f32[272,128]{1,0:T(8,128)S(1)}, u32[]{:S(2)}, u32[]{:S(2)}) collective-permute-start(f32[272,128]{1,0:T(8,128)S(1)} %pad_maximum_fusion.3), channel_id=1, source_target_pairs={{0,4},{4,0},{8,12},{12,8},{16,20},{20,16},{24,28},{28,24},{1,5},{5... | collective-permute-start | bytes 417800 | tf_op jit(solution)/shard_map/ppermute | solution.py:1085
  350.5 16.6 %collective-permute-start.49 = (f32[4,64,512]{2,1,0:T(8,128)S(1)}, f32[4,64,512]{2,1,0:T(8,128)S(1)}, u32[]{:S(2)}, u32[]{:S(2)}) collective-permute-start(f32[4,64,512]{2,1,0:T(8,128)S(1)} %pad_maximum_fusion.1.near), channel_id=1, source_target_pairs={{0,4},{4,0},{8,12},{12,8},{16,20},{20,16},{24,28},{28,24},{1,5},{5... | collective-permute-start | bytes 1572872 | tf_op jit(solution)/shard_map/ppermute | solution.py:1085
  354.6 9.1 %collective-permute-start.45 = (f32[272,128]{1,0:T(8,128)S(1)}, f32[272,128]{1,0:T(8,128)S(1)}, u32[]{:S(2)}, u32[]{:S(2)}) collective-permute-start(f32[272,128]{1,0:T(8,128)S(1)} %add.109), channel_id=1, source_target_pairs={{0,16},{4,20},{8,24},{12,28},{16,0},{20,4},{24,8},{28,12},{1,17},{... | collective-permute-start | bytes 417800 | tf_op jit(solution)/shard_map/ppermute | solution.py:1085
  (33 other events, 281.5 us)
Sparse Core Ops, SparseCore 0:
  18.4 50.8 all-gather.2
where the time goes:
time: 381 us; the launch traced here: 377 us
  Pallas kernels  258 us (68%)
  starting transfers between devices  72.3 us (19%)
  between operations  16.3 us (4%)
  waiting for transfers between devices  12.4 us (3%)
  local copies, waits for them, and re-layouts  10 us (3%)
  other arithmetic  8.07 us (2%)
    pallas_call x4, Pallas kernels, feed_call(): call(body, [specs[kind][0] for kind in outs], in_specs, [specs[kind][1] f...  93.9 us
    ppermute x50, starting transfers between devices, swap(): return lax.ppermute(value, axis, [(i, i ^ distance) for i in range(size)])  54.2 us
    pallas_call x2, Pallas kernels, weight_grads(): call(weight_body, [shape, shape], [SMEM, SMEM] + [wide] * 2 + [pl.BlockSp...  44.5 us
    pallas_call x1, Pallas kernels, mix_forward(): call(mix_body, [half, half] + [sds((4096, 256))] * 3, [re, im, whole((256...  22.3 us
    pallas_call x2, Pallas kernels, mix_backward(): call(mix_back_body, shapes, in_specs, out_specs, grid=(count // 2,), scra...  20.5 us
    pallas_call x1, Pallas kernels, first_stage(): call(first_body, [sds((SMAX, FREQ, LANES)), sds((SMAX, SMAX, LANES)), sds...  10.3 us
    pallas_call x1, Pallas kernels, last_back(): call(last_back_body, [sds((SMAX, SMAX, LANES)), sds((PACK, LANES))] + [sd...  9.68 us
    pallas_call x1, Pallas kernels, final_stage(): call(final_body, sds((SMAX, SMAX, LANES)), [SMEM, field, field, field, pl...  9.43 us
  transfers between devices with their start and end apart: 55, of which 7 were waited for; matrix products, arithmetic and copies ran while one was open for 3% of the time, Pallas kernels for 68%

commit v1 on v0

--- a/solution.py
+++ b/solution.py
@@ -37,6 +37,7 @@
 NT = (((1,), (1,)), ((), ()))
 TN = (((0,), (0,)), ((), ()))
 LIMIT = 56 * 1024 * 1024
+LESS = 32 * 1024 * 1024
 
 
 def mm(left, right, dims=NN):
@@ -107,7 +108,7 @@
     return (int(time * 1e9), int(time * 3e6))
 
 
-def call(body, out_shape, in_specs, out_specs, grid=(), scratch=(), aliases=None, cost=None):
+def call(body, out_shape, in_specs, out_specs, grid=(), scratch=(), aliases=None, cost=None, limit=LESS):
     flops, moved = cost or (0, 0)
     return pl.pallas_call(
         body,
@@ -117,7 +118,7 @@
         out_specs=out_specs,
         scratch_shapes=list(scratch),
         input_output_aliases=aliases or {},
-        compiler_params=pltpu.CompilerParams(vmem_limit_bytes=LIMIT),
+        compiler_params=pltpu.CompilerParams(vmem_limit_bytes=limit),
         cost_estimate=pl.CostEstimate(flops=flops, bytes_accessed=moved, transcendentals=0),
     )
 
@@ -741,6 +742,7 @@
         scratch=scratch,
         aliases=aliases,
         cost=us(cost),
+        limit=LIMIT,
     )(*args)
 
 
@@ -812,6 +814,7 @@
         grid=(4,),
         scratch=[pltpu.VMEM((C, rows), BF16)] * 2,
         cost=us(cost),
+        limit=LIMIT,
     )(own, place, th, tl, *left)
 
 

time: 381 us -> 387 us (1.016)
  local copies, waits for them, and re-layouts: 10 us -> 64.3 us
  Pallas kernels: 258 us -> 215 us
    unnamed x52 -> x164, local copies, waits for them, and re-layouts: 4.04 us -> 57.2 us
    pallas_call x2, Pallas kernels: 20.5 us -> 13.5 us  [mix_backward(): call(mix_back_body, shapes, in_specs, out_specs, grid=(count // 2,), scra...]
    pallas_call x2, Pallas kernels: 8.58 us -> 3.17 us  [last_stage(): call(last_body, [sds(shape)] * PARTS + [sds((SMAX, SMAX, LANES))], in_spe...]
    pallas_call x1, Pallas kernels: 9.68 us -> 4.73 us  [last_back(): call(last_back_body, [sds((SMAX, SMAX, LANES)), sds((PACK, LANES))] + [sd...]
    pallas_call x1, Pallas kernels: 9.43 us -> 4.98 us  [final_stage(): call(final_body, sds((SMAX, SMAX, LANES)), [SMEM, field, field, field, pl...]
  transfers between devices with their start and end apart: 55 -> 55, of which waited for: 7 -> 4; matrix products, arithmetic and copies ran while one was open for 3% -> 3% of each run, Pallas kernels for 68% -> 56%
where the time goes in v1:
time: 387 us; the launch traced here: 382 us
  Pallas kernels  215 us (56%)
  starting transfers between devices  68.7 us (18%)
  local copies, waits for them, and re-layouts  64.3 us (17%)
  between operations  16.7 us (4%)
  waiting for transfers between devices  10.4 us (3%)
  other arithmetic  6.85 us (2%)
    pallas_call x4, Pallas kernels, feed_call(): call(body, [specs[kind][0] for kind in outs], in_specs, [specs[kind][1] f...  93.5 us
    unnamed x164, local copies, waits for them, and re-layouts  57.2 us
    ppermute x50, starting transfers between devices, swap(): return lax.ppermute(value, axis, [(i, i ^ distance) for i in range(size)])  51.4 us
    pallas_call x2, Pallas kernels, weight_grads(): call(weight_body, [shape, shape], [SMEM, SMEM] + [wide] * 2 + [pl.BlockSp...  44.4 us
    pallas_call x1, Pallas kernels, mix_forward(): call(mix_body, [half, half] + [sds((4096, 256))] * 3, [re, im, whole((256...  19.7 us
    pallas_call x2, Pallas kernels, mix_backward(): call(mix_back_body, shapes, in_specs, out_specs, grid=(count // 2,), scra...  13.5 us
    ppermute x50, waiting for transfers between devices, swap(): return lax.ppermute(value, axis, [(i, i ^ distance) for i in range(size)])  9.08 us
  transfers between devices with their start and end apart: 55, of which 4 were waited for; matrix products, arithmetic and copies ran while one was open for 3% of the time, Pallas kernels for 56%

profile of v1, /device:TPU:0, one launch (start us, length us, event | category | flops | bytes accessed | tf_op | source)
XLA Modules:
  0.0 382.3 jit_solution(14450697018444083777)
XLA Ops:
  8.3 3.0 collective-permute-start.4
  11.9 2.3 copy-done.20
  16.3 2.1 shard_map.263.refs_0_.refs_10_.refs_9_
  22.8 2.3 copy-done.19
  25.2 3.3 shard_map.264
  34.0 4.9 %all-to-all-start = ((f32[4,2,8,96,128]{4,3,2,1,0:T(8,128)}), f32[4,2,8,96,128]{4,3,2,1,0:T(8,128)}, u32[]{:S(2)}, u32[]{:S(2)}) async-start(f32[4,2,8,96,128]{4,3,2,1,0:T(8,128)} %get-tuple-element.165), calls=%async_computation | async-start | bytes 6291456 | tf_op jit(solution)/shard_map/all_to_all | solution.py:1148
  39.0 2.3 copy-done.21
  41.3 7.2 %shard_map.266 = (f32[96,64,128]{2,1,0:T(8,128)S(1)}, f32[96,96,128]{2,1,0:T(8,128)S(1)}, f32[96,96,128]{2,1,0:T(8,128)S(1)}, f32[96,128]{1,0:T(8,128)S(1)}) custom-call(s32[1]{0:T(128)} %copy.62.side_ref, f32[96,96,128]{2,1,0:T(8,128)S(1)} %bitcast.110, f32[25,8,128]{2,1,0:T(8,128)S(1)} %shard_map.263.refs_0_.refs_10_.refs_9_, ...), custom_call_target="tpu_custom_call" | custom-call | flops 3000000000 | bytes 9000000 | tf_op jit(solution)/shard_map/pallas_call | solution.py:326
  48.5 2.2 copy-done
  50.7 2.1 copy-done.48
  53.4 19.7 %shard_map.267 = (f32[96,32,128]{2,1,0:T(8,128)S(1)}, f32[96,32,128]{2,1,0:T(8,128)S(1)}, f32[4096,256]{1,0:T(8,128)S(1)}, f32[4096,256]{1,0:T(8,128)S(1)}, f32[4096,256]{1,0:T(8,128)S(1)}) custom-call(f32[96,64,128]{2,1,0:T(8,128)S(1)} %get-tuple-element.157.re_ref.im_ref, f32[96,64,128]{2,1,0:T(8,128)S(1)} %get-tuple-element.157.re_ref.im_ref, ...), custom_call_target="tpu_custom_call" | custom-call | flops 100000000 | bytes 300000 | tf_op jit(solution)/shard_map/pallas_call | solution.py:420
  75.2 2.1 copy-done.24
  80.2 2.3 copy-done.1
  84.7 2.2 copy-done.3
  89.7 7.3 %shard_map.268 = (bf16[4,512,512]{2,1,0:T(8,128)(2,1)}, bf16[4,512,512]{2,1,0:T(8,128)(2,1)}, bf16[4,512,512]{2,1,0:T(8,128)(2,1)}, bf16[4,512,512]{2,1,0:T(8,128)(2,1)}) custom-call(s32[1]{0:T(128)} %bitcast.own_ref.refs_0_, f32[512,512]{1,0:T(8,128)} %refs_0_, f32[512,512]{1,0:T(8,128)} %collective-permute-done.3.refs_1_, f32[8,2,64,512]{3,2,1,0:T(8,128)} %bitcast.127, ...), custom_call_target="tpu_custom_call" | custom-call | flops 100000000 | bytes 300000 | tf_op jit(solution)/shard_map/pallas_call | solution.py:506
  97.0 2.3 copy-done.2
  99.3 2.3 copy-done.4
  104.4 2.2 copy-done.5
  109.6 28.5 %shard_map.271 = (bf16[2304,2048]{1,0:T(8,128)(2,1)}, bf16[2304,2048]{1,0:T(8,128)(2,1)}, bf16[2304,512]{1,0:T(8,128)(2,1)}, bf16[2304,512]{1,0:T(8,128)(2,1)}, ...) custom-call(s32[1]{0:T(128)} %bitcast.own_ref.refs_0_, ...), custom_call_target="tpu_custom_call" | custom-call | flops 28000000000 | bytes 84000000 | tf_op jit(solution)/shard_map/pallas_call | solution.py:736
  138.2 3.9 %all-to-all-start.1 = ((f32[4,1,8,96,128]{4,3,2,1,0:T(8,128)}), f32[4,1,8,96,128]{4,3,2,1,0:T(8,128)S(1)}, u32[]{:S(2)}, u32[]{:S(2)}) async-start(f32[4,1,8,96,128]{4,3,2,1,0:T(8,128)} %get-tuple-element.186), calls=%async_computation.1 | async-start | bytes 3145728 | tf_op jit(solution)/shard_map/all_to_all | solution.py:1176
  145.2 28.5 %shard_map.272 = (bf16[2304,2048]{1,0:T(8,128)(2,1)}, bf16[2304,2048]{1,0:T(8,128)(2,1)}, bf16[2304,512]{1,0:T(8,128)(2,1)}, bf16[2304,512]{1,0:T(8,128)(2,1)}, ...) custom-call(s32[1]{0:T(128)} %bitcast.own_ref.refs_0_, ...), custom_call_target="tpu_custom_call", output_to_operand_aliasing={{0}: (14, {}), {1}: (15, {}), {2}: (16, {}), {3}: (17, {}),... | custom-call | flops 28000000000 | bytes 84000000 | tf_op jit(solution)/shard_map/pallas_call | solution.py:736
  175.8 19.3 %shard_map.273 = (bf16[2304,2048]{1,0:T(8,128)(2,1)}, bf16[2304,2048]{1,0:T(8,128)(2,1)}, bf16[2304,512]{1,0:T(8,128)(2,1)}, bf16[2304,512]{1,0:T(8,128)(2,1)}, ...) custom-call(s32[1]{0:T(128)} %bitcast.own_ref.refs_0_, ...), custom_call_target="tpu_custom_call", output_to_operand_aliasing={{0}: (13, {}), {1}: (14, {}), {2}: (15, {}), {3}: (16, {})} | custom-call | flops 17999998976 | bytes 54000000 | tf_op jit(solution)/shard_map/pallas_call | solution.py:736
  195.1 3.7 all-to-all-start.3
  198.9 22.1 %shard_map.274 = (f32[2,8,64,512]{3,2,1,0:T(8,128)}, f32[2,8,64,512]{3,2,1,0:T(8,128)}) custom-call(s32[1]{0:T(128)} %bitcast.own_ref.refs_0_, s32[1]{0:T(128)} %bitcast.19.place_ref, bf16[2304,2048]{1,0:T(8,128)(2,1)} %get-tuple-element.202.th, bf16[2304,2048]{1,0:T(8,128)(2,1)} %get-tuple-element.203.tl, f32[4,1536,128]{2,1,0:T(8,128)} %bitcast.10.refs_5_.refs_0_, ...), custom_call_target="tpu_custom_call" | custom-call | flops 20000000000 | bytes 60000000 | tf_op jit(solution)/shard_map/pallas_call | solution.py:804
  221.4 17.1 %shard_map.275 = (bf16[2304,2048]{1,0:T(8,128)(2,1)}, bf16[2304,2048]{1,0:T(8,128)(2,1)}, f32[768,128]{1,0:T(8,128)}, f32[768,128]{1,0:T(8,128)}, f32[768,128]{1...) custom-call(s32[1]{0:T(128)} %bitcast.own_ref.refs_0_, ...), custom_call_target="tpu_custom_call", output_to_operand_aliasing={{0}: (13, {}), {1}: (14, {})} | custom-call | flops 16000000000 | bytes 48000000 | tf_op jit(solution)/shard_map/pallas_call | solution.py:736
  244.4 4.8 %all-to-all-start.2 = ((f32[4,1,768,128]{3,2,1,0:T(8,128)}), f32[4,1,768,128]{3,2,1,0:T(8,128)}, u32[]{:S(2)}, u32[]{:S(2)}) async-start(f32[4,1,768,128]{3,2,1,0:T(8,128)} %get-tuple-element.222), calls=%async_computation.2 | async-start | bytes 3145728 | tf_op jit(solution)/shard_map/all_to_all | solution.py:1193
  249.1 22.3 %shard_map.278 = (f32[2,8,64,512]{3,2,1,0:T(8,128)}, f32[2,8,64,512]{3,2,1,0:T(8,128)}) custom-call(s32[1]{0:T(128)} %bitcast.own_ref.refs_0_, s32[1]{0:T(128)} %bitcast.19.place_ref, bf16[2304,2048]{1,0:T(8,128)(2,1)} %get-tuple-element.236.th, bf16[2304,2048]{1,0:T(8,128)(2,1)} %get-tuple-element.237.tl, bf16[2304,512]{1,0:T(8,128)(2,1)} %get-tuple-element.238.refs_0_, ...), custom_call_target="tpu_custom_call" | custom-call | flops 20000000000 | bytes 60000000 | tf_op jit(solution)/shard_map/pallas_call | solution.py:804
  272.1 2.5 slice_add_fusion
  278.9 4.1 %shard_map.276 = (f32[96,64,128]{2,1,0:T(8,128)S(1)}, f32[96,96,128]{2,1,0:T(8,128)S(1)}) custom-call(s32[1]{0:T(128)} %bitcast.own_ref.refs_0_, bf16[64,768]{1,0:T(8,128)(2,1)S(1)} %copy-done.61, f32[8,96,128]{2,1,0:T(8,128)S(1)} %bitcast.123, f32[8,96,128]{2,1,0:T(8,128)S(1)} %bitcast.113, f32[8,96,128]{2,1,0:T(8,128)} %bitcast.26.refs_2_, ...), custom_call_target="tpu_custom_call" | custom-call | flops 8000000000 | bytes 24000000 | tf_op jit(solution)/shard_map/pallas_call | solution.py:861
  283.0 2.2 copy-done.51
  286.9 4.5 %shard_map.277 = f32[96,96,128]{2,1,0:T(8,128)} custom-call(s32[1]{0:T(128)} %copy.62.side_ref, f32[96,96,128]{2,1,0:T(8,128)S(1)} %bitcast.106, f32[4,2,8,96,128]{4,3,2,1,0:T(8,128)S(1)} %bitcast.107, f32[4,8,96,128]{3,2,1,0:T(8,128)} %bitcast.37.tip_ref, f32[1,128]{1,0:T(1,128)S(1)} %bitcast.119), custom_call_target="tpu_custom_call" | custom-call | flops 5000000000 | bytes 15000000 | tf_op jit(solution)/shard_map/pallas_call | solution.py:1069
  293.2 2.5 collective-permute-start.28
  295.8 2.2 add.93
  300.3 2.2 copy-done.27
  302.4 6.7 %shard_map.279 = (f32[96,16,128]{2,1,0:T(8,128)S(1)}, f32[96,16,128]{2,1,0:T(8,128)S(1)}, f32[256,256]{1,0:T(8,128)S(1)}, f32[256,256]{1,0:T(8,128)S(1)}, f32[8,256]{1,0:T(8,128)S(1)}, /*index=5*/f32[8,256]{1,0:T(8,128)S(1)}) custom-call(f32[96,64,128]{2,1,0:T(8,128)S(1)} %copy-done.55, f32[96,64,128]{2,1,0:T(8,128)S(1)} %copy-done.55, ...), custom_call_target="tpu_custom_call" | custom-call | flops 12999999488 | bytes 39000000 | tf_op jit(solution)/shard_map/pallas_call | solution.py:953
  309.2 2.8 collective-permute-start.33
  316.0 6.9 %shard_map.280 = (f32[96,16,128]{2,1,0:T(8,128)S(1)}, f32[96,16,128]{2,1,0:T(8,128)S(1)}, f32[264,128]{1,0:T(8,128)S(1)}) custom-call(f32[96,64,128]{2,1,0:T(8,128)S(1)} %copy-done.55, f32[96,64,128]{2,1,0:T(8,128)S(1)} %copy-done.55, f32[4096,256]{1,0:T(8,128)S(1)} %copy-done.23, f32[4096,256]{1,0:T(8,128)S(1)} %copy-done.25, f32[4096,256]{1,0:T(8,128)S(1)} %copy-done.27, ...), custom_call_target="tpu_custom_call" | custom-call | flops 12999999488 | bytes 39000000 | tf_op jit(solution)/shard_map/pallas_call | solution.py:953
  325.8 2.2 collective-permute-start.39
  328.4 2.3 copy-done.49
  330.7 2.3 copy-done.52
  333.1 4.7 %shard_map.281 = (f32[96,96,128]{2,1,0:T(8,128)S(1)}, f32[264,128]{1,0:T(8,128)S(1)}, f32[25,8,128]{2,1,0:T(8,128)S(1)}, f32[25,8,128]{2,1,0:T(8,128)S(1)}, f32[...) custom-call(f32[96,16,128]{2,1,0:T(8,128)S(1)} %get-tuple-element.249.re0, f32[96,16,128]{2,1,0:T(8,128)S(1)} %get-tuple-element.259.re1, ...), custom_call_target="tpu_custom_call" | custom-call | flops 12999999488 | bytes 39000000 | tf_op jit(solution)/shard_map/pallas_call | solution.py:1010
  339.8 2.7 collective-permute-start.48
  346.2 2.3 copy-done.50
  348.5 2.3 copy-done.53
  350.9 5.0 %shard_map.282 = f32[96,96,128]{2,1,0:T(8,128)} custom-call(s32[1]{0:T(128)} %copy.62.side_ref, f32[96,96,128]{2,1,0:T(8,128)S(1)} %copy-done.53, f32[96,96,128]{2,1,0:T(8,128)S(1)} %get-tuple-element.276.dn_ref, f32[96,96,128]{2,1,0:T(8,128)S(1)} %copy-done.50, f32[96,128]{1,0:T(8,128)S(1)} %copy-done.63, f32[1,128]{1,0:T(1,128)S(1)} %bitcast.122, ...), custom_call_target="tpu_custom_call" | custom-call | flops 12999999488 | bytes 39000000 | tf_op jit(solution)/shard_map/pallas_call | solution.py:1045
  358.8 2.9 collective-permute-done.44
  361.8 2.1 collective-permute-start.45
  365.3 5.5 %collective-permute-done.45 = f32[272,128]{1,0:T(8,128)S(1)} collective-permute-done((f32[272,128]{1,0:T(8,128)S(1)}, f32[272,128]{1,0:T(8,128)S(1)}, u32[]{:S(2)}, u32[]{:S(2)}) %collective-permute-start.45) | collective-permute-done | bytes 139296 | tf_op jit(solution)/shard_map/ppermute | solution.py:1088
  (292 shorter events, 72.2 us)
Async XLA Ops:
  7.2 72.1 %all-gather.3.cloned.1.call-start = ((), (), s32[]{:S(2)}) async-start(), calls=%async_computation.4 | async-start | bytes 2359296 | tf_op jit(solution)/shard_map/all_gather | solution.py:1151
  8.3 10.1 %collective-permute-start.4 = (f32[2,64,512]{2,1,0:T(8,128)S(1)}, f32[2,64,512]{2,1,0:T(8,128)S(1)}, u32[]{:S(2)}, u32[]{:S(2)}) collective-permute-start(f32[2,64,512]{2,1,0:T(8,128)S(1)} %pad_maximum_fusion.2), channel_id=1, source_target_pairs={{0,2},{1,3},{2,0},{3,1},{4,6},{5,7},{6,4},{7,5},{8,10},{9,11},{10,... | collective-permute-start | bytes 786440 | tf_op jit(solution)/shard_map/ppermute | solution.py:1088
  19.1 14.9 %collective-permute-start.2 = (f32[25,8,128]{2,1,0:T(8,128)S(1)}, f32[25,8,128]{2,1,0:T(8,128)S(1)}, u32[]{:S(2)}, u32[]{:S(2)}) collective-permute-start(f32[25,8,128]{2,1,0:T(8,128)S(1)} %shard_map.263.refs_0_.refs_10_.refs_9_), channel_id=1, source_target_pairs={{0,3},{1,2},{2,1},{3,0},{4,7},{5,6},{6,5},{7,4},{8,11},{9,10},{10,... | collective-permute-start | bytes 307208 | tf_op jit(solution)/shard_map/ppermute | solution.py:1088
  19.2 14.8 %collective-permute-start.1 = (f32[25,8,128]{2,1,0:T(8,128)S(1)}, f32[25,8,128]{2,1,0:T(8,128)S(1)}, u32[]{:S(2)}, u32[]{:S(2)}) collective-permute-start(f32[25,8,128]{2,1,0:T(8,128)S(1)} %shard_map.263.refs_0_.refs_10_.refs_9_), channel_id=1, source_target_pairs={{0,2},{1,3},{2,0},{3,1},{4,6},{5,7},{6,4},{7,5},{8,10},{9,11},{10,... | collective-permute-start | bytes 307208 | tf_op jit(solution)/shard_map/ppermute | solution.py:1088
  20.4 13.7 %collective-permute-start = (f32[25,8,128]{2,1,0:T(8,128)S(1)}, f32[25,8,128]{2,1,0:T(8,128)S(1)}, u32[]{:S(2)}, u32[]{:S(2)}) collective-permute-start(f32[25,8,128]{2,1,0:T(8,128)S(1)} %shard_map.263.refs_0_.refs_10_.refs_9_), channel_id=1, source_target_pairs={{0,1},{1,0},{2,3},{3,2},{4,5},{5,4},{6,7},{7,6},{8,9},{9,8},{10,11... | collective-permute-start | bytes 307208 | tf_op jit(solution)/shard_map/ppermute | solution.py:1088
  34.0 63.0 %all-to-all-start = ((f32[4,2,8,96,128]{4,3,2,1,0:T(8,128)}), f32[4,2,8,96,128]{4,3,2,1,0:T(8,128)}, u32[]{:S(2)}, u32[]{:S(2)}) async-start(f32[4,2,8,96,128]{4,3,2,1,0:T(8,128)} %get-tuple-element.165), calls=%async_computation | async-start | bytes 6291456 | tf_op jit(solution)/shard_map/all_to_all | solution.py:1148
  79.2 10.4 %collective-permute-start.5 = (f32[8,2,64,512]{3,2,1,0:T(8,128)}, f32[8,2,64,512]{3,2,1,0:T(8,128)}, u32[]{:S(2)}, u32[]{:S(2)}) collective-permute-start(f32[8,2,64,512]{3,2,1,0:T(8,128)} %bitcast.126), channel_id=1, source_target_pairs={{0,1},{1,0},{2,3},{3,2},{4,5},{5,4},{6,7},{7,6},{8,9},{9,8},{10,11... | collective-permute-start | bytes 6291464 | tf_op jit(solution)/shard_map/ppermute | solution.py:1088
  79.7 10.0 %collective-permute-start.3 = (f32[512,512]{1,0:T(8,128)}, f32[512,512]{1,0:T(8,128)}, u32[]{:S(2)}, u32[]{:S(2)}) collective-permute-start(f32[512,512]{1,0:T(8,128)} %refs_0_), channel_id=1, source_target_pairs={{0,1},{1,0},{2,3},{3,2},{4,5},{5,4},{6,7},{7,6},{8,9},{9,8},{10,11... | collective-permute-start | bytes 3145736 | tf_op jit(solution)/shard_map/ppermute | solution.py:1088
  79.8 9.9 %collective-permute-start.6 = (f32[512,512]{1,0:T(8,128)}, f32[512,512]{1,0:T(8,128)}, u32[]{:S(2)}, u32[]{:S(2)}) collective-permute-start(f32[512,512]{1,0:T(8,128)} %refs_4_), channel_id=1, source_target_pairs={{0,1},{1,0},{2,3},{3,2},{4,5},{5,4},{6,7},{7,6},{8,9},{9,8},{10,11... | collective-permute-start | bytes 3145736 | tf_op jit(solution)/shard_map/ppermute | solution.py:1088
  87.6 22.0 %collective-permute-start.7 = (f32[8,96,128]{2,1,0:T(8,128)}, f32[8,96,128]{2,1,0:T(8,128)}, u32[]{:S(2)}, u32[]{:S(2)}) collective-permute-start(f32[8,96,128]{2,1,0:T(8,128)} %get-tuple-element.180), channel_id=1, source_target_pairs={{0,1},{1,0},{2,3},{3,2},{4,5},{5,4},{6,7},{7,6},{8,9},{9,8},{10,11... | collective-permute-start | bytes 1179656 | tf_op jit(solution)/shard_map/ppermute | solution.py:1088
  87.7 21.9 %collective-permute-start.8 = (f32[8,96,128]{2,1,0:T(8,128)}, f32[8,96,128]{2,1,0:T(8,128)}, u32[]{:S(2)}, u32[]{:S(2)}) collective-permute-start(f32[8,96,128]{2,1,0:T(8,128)} %get-tuple-element.181), channel_id=1, source_target_pairs={{0,2},{1,3},{2,0},{3,1},{4,6},{5,7},{6,4},{7,5},{8,10},{9,11},{10,... | collective-permute-start | bytes 1179656 | tf_op jit(solution)/shard_map/ppermute | solution.py:1088
  89.7 19.9 %collective-permute-start.9 = (f32[8,96,128]{2,1,0:T(8,128)}, f32[8,96,128]{2,1,0:T(8,128)}, u32[]{:S(2)}, u32[]{:S(2)}) collective-permute-start(f32[8,96,128]{2,1,0:T(8,128)} %get-tuple-element.182), channel_id=1, source_target_pairs={{0,3},{1,2},{2,1},{3,0},{4,7},{5,6},{6,5},{7,4},{8,11},{9,10},{10,... | collective-permute-start | bytes 1179656 | tf_op jit(solution)/shard_map/ppermute | solution.py:1088
  107.5 36.9 %collective-permute-start.10 = (f32[2,8,96,128]{3,2,1,0:T(8,128)}, f32[2,8,96,128]{3,2,1,0:T(8,128)S(1)}, u32[]{:S(2)}, u32[]{:S(2)}) collective-permute-start(f32[2,8,96,128]{3,2,1,0:T(8,128)} %get-tuple-element.188), channel_id=1, source_target_pairs={{0,1},{1,0},{2,3},{3,2},{4,5},{5,4},{6,7},{7,6},{8,9},{9,8},{10,11... | collective-permute-start | bytes 2359304 | tf_op jit(solution)/shard_map/ppermute | solution.py:1088
  107.6 36.8 %collective-permute-start.11 = (f32[2,8,96,128]{3,2,1,0:T(8,128)}, f32[2,8,96,128]{3,2,1,0:T(8,128)}, u32[]{:S(2)}, u32[]{:S(2)}) collective-permute-start(f32[2,8,96,128]{3,2,1,0:T(8,128)} %get-tuple-element.189), channel_id=1, source_target_pairs={{0,2},{1,3},{2,0},{3,1},{4,6},{5,7},{6,4},{7,5},{8,10},{9,11},{10,... | collective-permute-start | bytes 2359304 | tf_op jit(solution)/shard_map/ppermute | solution.py:1088
  109.6 34.8 %collective-permute-start.12 = (f32[2,8,96,128]{3,2,1,0:T(8,128)}, f32[2,8,96,128]{3,2,1,0:T(8,128)}, u32[]{:S(2)}, u32[]{:S(2)}) collective-permute-start(f32[2,8,96,128]{3,2,1,0:T(8,128)} %get-tuple-element.190), channel_id=1, source_target_pairs={{0,3},{1,2},{2,1},{3,0},{4,7},{5,6},{6,5},{7,4},{8,11},{9,10},{10,... | collective-permute-start | bytes 2359304 | tf_op jit(solution)/shard_map/ppermute | solution.py:1088
  138.2 37.0 %all-to-all-start.1 = ((f32[4,1,8,96,128]{4,3,2,1,0:T(8,128)}), f32[4,1,8,96,128]{4,3,2,1,0:T(8,128)S(1)}, u32[]{:S(2)}, u32[]{:S(2)}) async-start(f32[4,1,8,96,128]{4,3,2,1,0:T(8,128)} %get-tuple-element.186), calls=%async_computation.1 | async-start | bytes 3145728 | tf_op jit(solution)/shard_map/all_to_all | solution.py:1176
  142.1 33.1 %collective-permute-start.13 = (f32[768,128]{1,0:T(8,128)S(1)}, f32[768,128]{1,0:T(8,128)S(1)}, u32[]{:S(2)}, u32[]{:S(2)}) collective-permute-start(f32[768,128]{1,0:T(8,128)S(1)} %copy-done.79), channel_id=1, source_target_pairs={{0,1},{1,0},{2,3},{3,2},{4,5},{5,4},{6,7},{7,6},{8,9},{9,8},{10,11... | collective-permute-start | bytes 1179656 | tf_op jit(solution)/shard_map/ppermute | solution.py:1088
  142.7 56.2 %collective-permute-start.14 = (f32[768,128]{1,0:T(8,128)}, f32[768,128]{1,0:T(8,128)}, u32[]{:S(2)}, u32[]{:S(2)}) collective-permute-start(f32[768,128]{1,0:T(8,128)} %get-tuple-element.205), channel_id=1, source_target_pairs={{0,2},{1,3},{2,0},{3,1},{4,6},{5,7},{6,4},{7,5},{8,10},{9,11},{10,... | collective-permute-start | bytes 1179656 | tf_op jit(solution)/shard_map/ppermute | solution.py:1088
  144.3 54.5 %collective-permute-start.15 = (f32[768,128]{1,0:T(8,128)}, f32[768,128]{1,0:T(8,128)}, u32[]{:S(2)}, u32[]{:S(2)}) collective-permute-start(f32[768,128]{1,0:T(8,128)} %get-tuple-element.206), channel_id=1, source_target_pairs={{0,3},{1,2},{2,1},{3,0},{4,7},{5,6},{6,5},{7,4},{8,11},{9,10},{10,... | collective-permute-start | bytes 1179656 | tf_op jit(solution)/shard_map/ppermute | solution.py:1088
  173.7 25.1 %collective-permute-start.16 = (f32[768,128]{1,0:T(8,128)}, f32[768,128]{1,0:T(8,128)}, u32[]{:S(2)}, u32[]{:S(2)}) collective-permute-start(f32[768,128]{1,0:T(8,128)} %get-tuple-element.207), channel_id=1, source_target_pairs={{0,1},{1,0},{2,3},{3,2},{4,5},{5,4},{6,7},{7,6},{8,9},{9,8},{10,11... | collective-permute-start | bytes 1179656 | tf_op jit(solution)/shard_map/ppermute | solution.py:1088
  173.9 25.0 %collective-permute-start.17 = (f32[768,128]{1,0:T(8,128)}, f32[768,128]{1,0:T(8,128)}, u32[]{:S(2)}, u32[]{:S(2)}) collective-permute-start(f32[768,128]{1,0:T(8,128)} %get-tuple-element.208), channel_id=1, source_target_pairs={{0,2},{1,3},{2,0},{3,1},{4,6},{5,7},{6,4},{7,5},{8,10},{9,11},{10,... | collective-permute-start | bytes 1179656 | tf_op jit(solution)/shard_map/ppermute | solution.py:1088
  175.2 23.6 %collective-permute-start.18 = (f32[768,128]{1,0:T(8,128)}, f32[768,128]{1,0:T(8,128)}, u32[]{:S(2)}, u32[]{:S(2)}) collective-permute-start(f32[768,128]{1,0:T(8,128)} %get-tuple-element.209), channel_id=1, source_target_pairs={{0,3},{1,2},{2,1},{3,0},{4,7},{5,6},{6,5},{7,4},{8,11},{9,10},{10,... | collective-permute-start | bytes 1179656 | tf_op jit(solution)/shard_map/ppermute | solution.py:1088
  195.1 49.3 %all-to-all-start.3 = ((f32[4,2,768,128]{3,2,1,0:T(8,128)}), f32[4,2,768,128]{3,2,1,0:T(8,128)S(1)}, u32[]{:S(2)}, u32[]{:S(2)}) async-start(f32[4,2,768,128]{3,2,1,0:T(8,128)} %get-tuple-element.232), calls=%async_computation.3 | async-start | bytes 6291456 | tf_op jit(solution)/shard_map/all_to_all | solution.py:1182
  221.0 19.7 %collective-permute-start.19 = (f32[2,8,64,512]{3,2,1,0:T(8,128)}, f32[2,8,64,512]{3,2,1,0:T(8,128)S(1)}, u32[]{:S(2)}, u32[]{:S(2)}) collective-permute-start(f32[2,8,64,512]{3,2,1,0:T(8,128)} %get-tuple-element.220), channel_id=1, source_target_pairs={{0,1},{1,0},{2,3},{3,2},{4,5},{5,4},{6,7},{7,6},{8,9},{9,8},{10,11... | collective-permute-start | bytes 6291464 | tf_op jit(solution)/shard_map/ppermute | solution.py:1088
  238.6 33.4 %collective-permute-start.21 = (f32[768,128]{1,0:T(8,128)}, f32[768,128]{1,0:T(8,128)}, u32[]{:S(2)}, u32[]{:S(2)}) collective-permute-start(f32[768,128]{1,0:T(8,128)} %get-tuple-element.226), channel_id=1, source_target_pairs={{0,1},{1,0},{2,3},{3,2},{4,5},{5,4},{6,7},{7,6},{8,9},{9,8},{10,11... | collective-permute-start | bytes 1179656 | tf_op jit(solution)/shard_map/ppermute | solution.py:1088
  238.7 33.3 %collective-permute-start.22 = (f32[768,128]{1,0:T(8,128)}, f32[768,128]{1,0:T(8,128)}, u32[]{:S(2)}, u32[]{:S(2)}) collective-permute-start(f32[768,128]{1,0:T(8,128)} %get-tuple-element.227), channel_id=1, source_target_pairs={{0,2},{1,3},{2,0},{3,1},{4,6},{5,7},{6,4},{7,5},{8,10},{9,11},{10,... | collective-permute-start | bytes 1179656 | tf_op jit(solution)/shard_map/ppermute | solution.py:1088
  240.7 31.4 %collective-permute-start.23 = (f32[768,128]{1,0:T(8,128)}, f32[768,128]{1,0:T(8,128)}, u32[]{:S(2)}, u32[]{:S(2)}) collective-permute-start(f32[768,128]{1,0:T(8,128)} %get-tuple-element.228), channel_id=1, source_target_pairs={{0,3},{1,2},{2,1},{3,0},{4,7},{5,6},{6,5},{7,4},{8,11},{9,10},{10,... | collective-permute-start | bytes 1179656 | tf_op jit(solution)/shard_map/ppermute | solution.py:1088
  242.9 29.2 %collective-permute-start.20 = (f32[2,4,64,512]{3,2,1,0:T(8,128)}, f32[2,4,64,512]{3,2,1,0:T(8,128)}, u32[]{:S(2)}, u32[]{:S(2)}) collective-permute-start(f32[2,4,64,512]{3,2,1,0:T(8,128)} %slice.150), channel_id=1, source_target_pairs={{0,4},{4,0},{8,12},{12,8},{16,20},{20,16},{24,28},{28,24},{1,5},{5... | collective-permute-start | bytes 3145736 | tf_op jit(solution)/shard_map/ppermute | solution.py:1088
  244.4 31.4 %all-to-all-start.2 = ((f32[4,1,768,128]{3,2,1,0:T(8,128)}), f32[4,1,768,128]{3,2,1,0:T(8,128)}, u32[]{:S(2)}, u32[]{:S(2)}) async-start(f32[4,1,768,128]{3,2,1,0:T(8,128)} %get-tuple-element.222), calls=%async_computation.2 | async-start | bytes 3145728 | tf_op jit(solution)/shard_map/all_to_all | solution.py:1193
  271.5 24.3 %collective-permute-start.25 = (f32[2,8,64,512]{3,2,1,0:T(8,128)}, f32[2,8,64,512]{3,2,1,0:T(8,128)}, u32[]{:S(2)}, u32[]{:S(2)}) collective-permute-start(f32[2,8,64,512]{3,2,1,0:T(8,128)} %get-tuple-element.242), channel_id=1, source_target_pairs={{0,1},{1,0},{2,3},{3,2},{4,5},{5,4},{6,7},{7,6},{8,9},{9,8},{10,11... | collective-permute-start | bytes 6291464 | tf_op jit(solution)/shard_map/ppermute | solution.py:1088
  277.1 14.4 %collective-permute-start.24 = (f32[4,64,512]{2,1,0:T(8,128)S(1)}, f32[4,64,512]{2,1,0:T(8,128)S(1)}, u32[]{:S(2)}, u32[]{:S(2)}) collective-permute-start(f32[4,64,512]{2,1,0:T(8,128)S(1)} %get-tuple-element.290), channel_id=1, source_target_pairs={{0,2},{1,3},{2,0},{3,1},{4,6},{5,7},{6,4},{7,5},{8,10},{9,11},{10,... | collective-permute-start | bytes 1572872 | tf_op jit(solution)/shard_map/ppermute | solution.py:1088
  291.6 17.5 %collective-permute-start.26 = (f32[64,512]{1,0:T(8,128)S(1)}, f32[64,512]{1,0:T(8,128)S(1)}, u32[]{:S(2)}, u32[]{:S(2)}) collective-permute-start(f32[64,512]{1,0:T(8,128)S(1)} %get-tuple-element.300), channel_id=1, source_target_pairs={{0,8},{4,12},{8,0},{12,4},{16,24},{20,28},{24,16},{28,20},{1,9},{5... | collective-permute-start | bytes 393224 | tf_op jit(solution)/shard_map/ppermute | solution.py:1088
  293.2 15.9 %collective-permute-start.28 = (f32[64,512]{1,0:T(8,128)S(1)}, f32[64,512]{1,0:T(8,128)S(1)}, u32[]{:S(2)}, u32[]{:S(2)}) collective-permute-start(f32[64,512]{1,0:T(8,128)S(1)} %get-tuple-element.301), channel_id=1, source_target_pairs={{0,24},{4,28},{8,16},{12,20},{16,8},{20,12},{24,0},{28,4},{1,25},{... | collective-permute-start | bytes 393224 | tf_op jit(solution)/shard_map/ppermute | solution.py:1088
  295.7 13.5 %collective-permute-start.27 = (f32[64,512]{1,0:T(8,128)S(1)}, f32[64,512]{1,0:T(8,128)S(1)}, u32[]{:S(2)}, u32[]{:S(2)}) collective-permute-start(f32[64,512]{1,0:T(8,128)S(1)} %get-tuple-element.302), channel_id=1, source_target_pairs={{0,16},{4,20},{8,24},{12,28},{16,0},{20,4},{24,8},{28,12},{1,17},{... | collective-permute-start | bytes 393224 | tf_op jit(solution)/shard_map/ppermute | solution.py:1088
  298.1 15.5 %collective-permute-start.29 = (f32[2,4,32,512]{3,2,1,0:T(8,128)S(1)}, f32[2,4,32,512]{3,2,1,0:T(8,128)S(1)}, u32[]{:S(2)}, u32[]{:S(2)}) collective-permute-start(f32[2,4,32,512]{3,2,1,0:T(8,128)S(1)} %slice.153), channel_id=1, source_target_pairs={{0,4},{4,0},{8,12},{12,8},{16,20},{20,16},{24,28},{28,24},{1,5},{5... | collective-permute-start | bytes 1572872 | tf_op jit(solution)/shard_map/ppermute | solution.py:1088
  299.7 14.1 %collective-permute-start.30 = (f32[8,32,512]{2,1,0:T(8,128)S(1)}, f32[8,32,512]{2,1,0:T(8,128)S(1)}, u32[]{:S(2)}, u32[]{:S(2)}) collective-permute-start(f32[8,32,512]{2,1,0:T(8,128)S(1)} %slice_bitcast_fusion), channel_id=1, source_target_pairs={{0,2},{1,3},{2,0},{3,1},{4,6},{5,7},{6,4},{7,5},{8,10},{9,11},{10,... | collective-permute-start | bytes 1572872 | tf_op jit(solution)/shard_map/ppermute | solution.py:1088
  309.2 13.8 %collective-permute-start.33 = (f32[64,512]{1,0:T(8,128)S(1)}, f32[64,512]{1,0:T(8,128)S(1)}, u32[]{:S(2)}, u32[]{:S(2)}) collective-permute-start(f32[64,512]{1,0:T(8,128)S(1)} %add_add_fusion.1), channel_id=1, source_target_pairs={{0,24},{4,28},{8,16},{12,20},{16,8},{20,12},{24,0},{28,4},{1,25},{... | collective-permute-start | bytes 393224 | tf_op jit(solution)/shard_map/ppermute | solution.py:1088
  312.0 11.0 %collective-permute-start.32 = (f32[64,512]{1,0:T(8,128)S(1)}, f32[64,512]{1,0:T(8,128)S(1)}, u32[]{:S(2)}, u32[]{:S(2)}) collective-permute-start(f32[64,512]{1,0:T(8,128)S(1)} %add_add_fusion.1), channel_id=1, source_target_pairs={{0,16},{4,20},{8,24},{12,28},{16,0},{20,4},{24,8},{28,12},{1,17},{... | collective-permute-start | bytes 393224 | tf_op jit(solution)/shard_map/ppermute | solution.py:1088
  312.6 10.4 %collective-permute-start.31 = (f32[64,512]{1,0:T(8,128)S(1)}, f32[64,512]{1,0:T(8,128)S(1)}, u32[]{:S(2)}, u32[]{:S(2)}) collective-permute-start(f32[64,512]{1,0:T(8,128)S(1)} %add_add_fusion.1), channel_id=1, source_target_pairs={{0,8},{4,12},{8,0},{12,4},{16,24},{20,28},{24,16},{28,20},{1,9},{5... | collective-permute-start | bytes 393224 | tf_op jit(solution)/shard_map/ppermute | solution.py:1088
  313.9 10.7 %collective-permute-start.35 = (f32[4,32,512]{2,1,0:T(8,128)S(1)}, f32[4,32,512]{2,1,0:T(8,128)S(1)}, u32[]{:S(2)}, u32[]{:S(2)}) collective-permute-start(f32[4,32,512]{2,1,0:T(8,128)S(1)} %get-tuple-element.298), channel_id=1, source_target_pairs={{0,2},{1,3},{2,0},{3,1},{4,6},{5,7},{6,4},{7,5},{8,10},{9,11},{10,... | collective-permute-start | bytes 786440 | tf_op jit(solution)/shard_map/ppermute | solution.py:1088
  323.1 23.1 %collective-permute-start.34 = (f32[4,64,512]{2,1,0:T(8,128)S(1)}, f32[4,64,512]{2,1,0:T(8,128)S(1)}, u32[]{:S(2)}, u32[]{:S(2)}) collective-permute-start(f32[4,64,512]{2,1,0:T(8,128)S(1)} %pad_maximum_fusion.near), channel_id=1, source_target_pairs={{0,4},{4,0},{8,12},{12,8},{16,20},{20,16},{24,28},{28,24},{1,5},{5... | collective-permute-start | bytes 1572872 | tf_op jit(solution)/shard_map/ppermute | solution.py:1088
  324.8 13.0 %collective-permute-start.37 = (f32[64,512]{1,0:T(8,128)S(1)}, f32[64,512]{1,0:T(8,128)S(1)}, u32[]{:S(2)}, u32[]{:S(2)}) collective-permute-start(f32[64,512]{1,0:T(8,128)S(1)} %get-tuple-element.292), channel_id=1, source_target_pairs={{0,8},{4,12},{8,0},{12,4},{16,24},{20,28},{24,16},{28,20},{1,9},{5... | collective-permute-start | bytes 393224 | tf_op jit(solution)/shard_map/ppermute | solution.py:1088
  325.8 12.0 %collective-permute-start.39 = (f32[64,512]{1,0:T(8,128)S(1)}, f32[64,512]{1,0:T(8,128)S(1)}, u32[]{:S(2)}, u32[]{:S(2)}) collective-permute-start(f32[64,512]{1,0:T(8,128)S(1)} %get-tuple-element.294), channel_id=1, source_target_pairs={{0,24},{4,28},{8,16},{12,20},{16,8},{20,12},{24,0},{28,4},{1,25},{... | collective-permute-start | bytes 393224 | tf_op jit(solution)/shard_map/ppermute | solution.py:1088
  339.8 17.4 %collective-permute-start.48 = (f32[64,512]{1,0:T(8,128)S(1)}, f32[64,512]{1,0:T(8,128)S(1)}, u32[]{:S(2)}, u32[]{:S(2)}) collective-permute-start(f32[64,512]{1,0:T(8,128)S(1)} %add_add_fusion), channel_id=1, source_target_pairs={{0,24},{4,28},{8,16},{12,20},{16,8},{20,12},{24,0},{28,4},{1,25},{... | collective-permute-start | bytes 393224 | tf_op jit(solution)/shard_map/ppermute | solution.py:1088
  342.5 14.7 %collective-permute-start.47 = (f32[64,512]{1,0:T(8,128)S(1)}, f32[64,512]{1,0:T(8,128)S(1)}, u32[]{:S(2)}, u32[]{:S(2)}) collective-permute-start(f32[64,512]{1,0:T(8,128)S(1)} %add_add_fusion), channel_id=1, source_target_pairs={{0,16},{4,20},{8,24},{12,28},{16,0},{20,4},{24,8},{28,12},{1,17},{... | collective-permute-start | bytes 393224 | tf_op jit(solution)/shard_map/ppermute | solution.py:1088
  343.7 13.5 %collective-permute-start.46 = (f32[64,512]{1,0:T(8,128)S(1)}, f32[64,512]{1,0:T(8,128)S(1)}, u32[]{:S(2)}, u32[]{:S(2)}) collective-permute-start(f32[64,512]{1,0:T(8,128)S(1)} %add_add_fusion), channel_id=1, source_target_pairs={{0,8},{4,12},{8,0},{12,4},{16,24},{20,28},{24,16},{28,20},{1,9},{5... | collective-permute-start | bytes 393224 | tf_op jit(solution)/shard_map/ppermute | solution.py:1088
  345.6 10.2 %collective-permute-start.43 = (f32[272,128]{1,0:T(8,128)S(1)}, f32[272,128]{1,0:T(8,128)S(1)}, u32[]{:S(2)}, u32[]{:S(2)}) collective-permute-start(f32[272,128]{1,0:T(8,128)S(1)} %pad_maximum_fusion.3), channel_id=1, source_target_pairs={{0,4},{4,0},{8,12},{12,8},{16,20},{20,16},{24,28},{28,24},{1,5},{5... | collective-permute-start | bytes 417800 | tf_op jit(solution)/shard_map/ppermute | solution.py:1088
  357.3 16.9 %collective-permute-start.49 = (f32[4,64,512]{2,1,0:T(8,128)S(1)}, f32[4,64,512]{2,1,0:T(8,128)S(1)}, u32[]{:S(2)}, u32[]{:S(2)}) collective-permute-start(f32[4,64,512]{2,1,0:T(8,128)S(1)} %pad_maximum_fusion.1.near), channel_id=1, source_target_pairs={{0,4},{4,0},{8,12},{12,8},{16,20},{20,16},{24,28},{28,24},{1,5},{5... | collective-permute-start | bytes 1572872 | tf_op jit(solution)/shard_map/ppermute | solution.py:1088
  (89 other events, 516.0 us)
Sparse Core Ops, SparseCore 0:
  19.2 49.9 all-gather.2
